TPU v7x, 32 devices: a whole 2x2x4 slice. The times are simulated.
32 devices in a mesh: region: 8 (over z, core), state: 4 (over y, x).
Axes of the slice: x: 2, y: 2, z: 4, core: 2. Of those that a mesh axis runs over, the one named last changes fastest.
Arguments:
- state_anom: float32 [8, 16, 256, 512], P('region', 'state'), may hold values from -6 to 6
- obs_anom: float32 [8, 256, 512], P('region', 'state'), may hold values from -6 to 6
- obs_weight: float32 [8, 256, 512], P('region', 'state'), may hold values from -6 to 6
- obs_cell: int32 [8, 256], P('region', 'state'), may hold values from 0 to 255, as said below
- sector_of: int32 [8], replicated, may hold values from 0 to 7, as said below
Outputs:
- increment: float32 [8, 16, 256, 512], P('region', 'state')
Inputs may be any that keep to these rules, and one draw needn't show every extreme that they name: `obs_cell`: each entry is lon * 8 + lat with lon in 0..31 and lat in 0..7. Within each aligned block of 64 entries along the observation dimension the entries do not decrease; in each such block between 8 and 16 entries have lon < 8, and between 8 and 16 have lon >= 24; the bound 16 is reached on both sides in every draw. `sector_of`: A permutation: every region holds a different sector.
All inputs are finite; a program needn't handle non-finite values.
Results may differ from a plain program's by a relative error of at most 0.0003.
Values sent between devices are 32-bit elements; how exact they have to be, the bound alone decides.
No kernel may reach another device: no remote copies, remote signals or barrier semaphores. Data moves between devices by JAX's collectives and lax.ppermute only.
A program may use at most 64 MiB of HBM per device.

v0:
```python
import functools

import jax
import jax.numpy as jnp
from jax import lax
from jax.experimental import pallas as pl
from jax.experimental.pallas import tpu as pltpu
from jax.sharding import PartitionSpec as P


SECT_W = 32
LAT = 8
HALF = 4
CAP = 16
EDGE = 2 * HALF * LAT
SUB = 8
LANES = 128
VMEM = pl.BlockSpec(memory_space=pltpu.VMEM)
SMEM = pl.BlockSpec(memory_space=pltpu.SMEM)
HBM = pl.BlockSpec(memory_space=pltpu.HBM)


def limit(mib):
    return pltpu.CompilerParams(vmem_limit_bytes=mib << 20)


def in_hbm(*values):
    return [pltpu.with_memory_space_constraint(value, pltpu.HBM) for value in values]


def partner(index, step, size):
    return index ^ step if size & (size - 1) == 0 else (index + size - step) % size


def target(index, step, size):
    return index ^ step if size & (size - 1) == 0 else (index + step) % size


def exchange(value, axis, step):
    size = lax.axis_size(axis)
    return lax.ppermute(value, axis, [(i, target(i, step, size)) for i in range(size)])


def gaspari(scaled):
    inside = scaled * scaled * (scaled * (scaled * (0.5 - 0.25 * scaled) + 0.625) - 5.0 / 3.0) + 1.0
    floored = jnp.maximum(scaled, 1.0)
    outside = (
        scaled * (scaled * (scaled * (scaled * (scaled / 12.0 - 0.5) + 0.625) + 5.0 / 3.0) - 5.0)
        + 4.0
        - 2.0 / (3.0 * floored)
    )
    return jnp.where(scaled <= 1.0, inside, jnp.where(scaled < 2.0, outside, 0.0))


def taper(first_col, rows, cells, lon_shift):
    cols = first_col + lax.broadcasted_iota(jnp.int32, (rows, cells.shape[1]), 0)
    obs = cells.astype(jnp.int32)
    lon_gap = cols // LAT - (obs // LAT + lon_shift)
    lat_gap = cols % LAT - obs % LAT
    scaled = jnp.sqrt((lon_gap * lon_gap + lat_gap * lat_gap).astype(jnp.float32)) / HALF
    return gaspari(scaled)


def split(value):
    high = value.astype(jnp.bfloat16)
    return high, (value - high.astype(jnp.float32)).astype(jnp.bfloat16)


def product(left, right, dims):
    dot = functools.partial(lax.dot_general, dimension_numbers=(dims, ((), ())), preferred_element_type=jnp.float32)
    return dot(left[0], right[0]) + (dot(left[0], right[1]) + dot(left[1], right[0]))


NT = ((1,), (1,))
NN = ((1,), (0,))


def folded(rows):
    return jnp.concatenate([rows[i : i + SUB] for i in range(0, rows.shape[0], SUB)], axis=1)


def unfolded(tiles, members):
    return jnp.concatenate([tiles[:, i : i + members] for i in range(0, tiles.shape[1], members)], axis=0)


def pack_kernel(sector_hbm, anom_hbm, weight_hbm, cell_hbm, own_ref, *refs):
    side_ref, *slot_refs, sector_ref, anom_ref, weight_ref, cell_ref, sems = refs
    count, members = weight_ref.shape
    loads = [
        pltpu.make_async_copy(cell_hbm, cell_ref, sems.at[0]),
        pltpu.make_async_copy(sector_hbm, sector_ref, sems.at[1]),
        pltpu.make_async_copy(weight_hbm.at[0], weight_ref, sems.at[2]),
        pltpu.make_async_copy(anom_hbm.at[0], anom_ref, sems.at[3]),
    ]
    for load in loads:
        load.start()
    regions = lax.axis_size("region")
    me = lax.axis_index("region")
    entry = lax.broadcasted_iota(jnp.int32, (count, LANES), 0)
    lane = lax.broadcasted_iota(jnp.int32, (count, LANES), 1)
    picks = [
        jnp.where(entry == start + lane % width, 1.0, 0.0).astype(jnp.bfloat16)
        for start, width in ((0, count), (0, CAP), (count - CAP, CAP))
    ]
    loads[0].wait()
    cells = jnp.broadcast_to(cell_ref[...].astype(jnp.float32), (SUB, count)).astype(jnp.bfloat16)
    spread = [lax.dot_general(cells, pick, (NN, ((), ())), preferred_element_type=jnp.float32) for pick in picks]
    loads[1].wait()
    mine = sector_ref[me]
    to_right, from_left, from_right = [], jnp.int32(0), jnp.int32(0)
    for step in range(1, regions):
        to_right.append(sector_ref[target(me, step, regions)] == lax.rem(mine + 1, regions))
        sector = sector_ref[partner(me, step, regions)]
        from_left = jnp.where(sector == lax.rem(mine + regions - 1, regions), step, from_left)
        from_right = jnp.where(sector == lax.rem(mine + 1, regions), step, from_right)
    side_ref[0] = jnp.broadcast_to(from_left, (SUB, LANES))
    side_ref[1] = jnp.broadcast_to(from_right, (SUB, LANES))
    for load in loads[2:]:
        load.wait()
    half = count // SUB * members
    own_ref[:, :half] = folded(anom_ref[...])
    own_ref[:, half : 2 * half] = folded(weight_ref[...])
    own_ref[:, 2 * half :] = spread[0]
    low = (folded(anom_ref[:CAP, :]), folded(weight_ref[:CAP, :]), spread[1])
    high = (folded(anom_ref[count - CAP :, :]), folded(weight_ref[count - CAP :, :]), spread[2])
    wide = CAP // SUB * members
    for slot, up in zip(slot_refs, to_right):
        for (start, stop), lo, hi in zip(((0, wide), (wide, 2 * wide), (2 * wide, 2 * wide + LANES)), low, high):
            slot[:, start:stop] = jnp.where(up, hi, lo)


def pick_kernel(side_ref, *refs):
    *slot_refs, halo_ref = refs
    width = slot_refs[0].shape[1]
    for side in range(2):
        step_of = side_ref[side]
        for at in range(0, width, LANES):
            value = slot_refs[0][:, at : at + LANES]
            for step, slot in enumerate(slot_refs[1:], start=2):
                value = jnp.where(step_of == step, slot[:, at : at + LANES], value)
            halo_ref[:, side * width + at : side * width + at + LANES] = value


def own_kernel(blocks, state_hbm, *refs):
    pack_refs, (out_hbm, state_ref, out_ref, a_hi, a_lo, w_hi, w_lo, rho_ref, in_sem, out_sem) = refs[:blocks], refs[blocks:]
    levels, rows, members = state_ref.shape
    half = pack_refs[0].shape[1] // 2 // LANES * LANES
    count = half // members * SUB
    loads = [pltpu.make_async_copy(state_hbm.at[l], state_ref.at[l], in_sem.at[l]) for l in range(levels)]
    for load in loads:
        load.start()
    lane = lax.broadcasted_iota(jnp.int32, (1, LANES), 1)
    tiles = [pack[:1, 2 * half :] for pack in pack_refs]
    for b in range(blocks):
        here = pl.ds(b * count, count)
        a_hi[here, :], a_lo[here, :] = split(unfolded(pack_refs[b][:, :half], members))
        w_hi[here, :], w_lo[here, :] = split(unfolded(pack_refs[b][:, half : 2 * half], members))
    each = LANES // count
    for g in range(0, blocks, each):
        cells = tiles[g]
        for b in range(1, each):
            cells = jnp.where(lane >= b * count, tiles[g + b], cells)
        rho_ref[:, g * count : g * count + LANES] = taper(0, rows, cells, 0) / (members - 1)
    stores = []
    for l in range(levels):
        loads[l].wait()
        covar = product(split(state_ref[l]), (a_hi[...], a_lo[...]), NT) * rho_ref[...]
        out_ref[l] = product(split(covar), (w_hi[...], w_lo[...]), NN)
        stores.append(pltpu.make_async_copy(out_ref.at[l], out_hbm.at[l], out_sem.at[l]))
        stores[-1].start()
    for store in stores:
        store.wait()


def halo_kernel(blocks, total_ref, state_ref, *refs):
    halo_refs, (out_ref, total_buf, state_buf, in_sem, state_sem, out_sem) = refs[:blocks], refs[blocks:]
    levels, columns, members = state_ref.shape
    wide = CAP // SUB * members
    width = halo_refs[0].shape[1] // 2
    starts = (0, columns - EDGE)
    loads = [
        (
            pltpu.make_async_copy(total_ref.at[l, pl.ds(c, EDGE)], total_buf.at[s, pl.ds(l * EDGE, EDGE)], in_sem.at[s, l]),
            pltpu.make_async_copy(state_ref.at[l, pl.ds(c, EDGE)], state_buf.at[s, pl.ds(l * EDGE, EDGE)], state_sem.at[s, l]),
        )
        for s, c in enumerate(starts)
        for l in range(levels)
    ]
    for total_load, state_load in loads:
        state_load.start()
        total_load.start()
    lane = lax.broadcasted_iota(jnp.int32, (1, LANES), 1)
    per = LANES // CAP
    parts = []
    for s, shift in enumerate((-SECT_W, SECT_W)):
        at = s * width
        anom = split(jnp.concatenate([unfolded(h[:, at : at + wide], members) for h in halo_refs], axis=0))
        weight = split(jnp.concatenate([unfolded(h[:, at + wide : at + 2 * wide], members) for h in halo_refs], axis=0))
        tiles = [h[:1, at + 2 * wide : at + width] for h in halo_refs]
        groups = []
        for g in range(0, blocks, per):
            cells = tiles[g]
            for b in range(1, min(per, blocks - g)):
                cells = jnp.where(lane >= b * CAP, tiles[g + b], cells)
            groups.append(cells)
        cells = jnp.concatenate(groups, axis=1)[:, : blocks * CAP]
        parts.append((anom, weight, taper(starts[s], EDGE, cells, shift) / (members - 1)))
    for _, state_load in loads:
        state_load.wait()
    deltas = []
    for s, (anom, weight, rho) in enumerate(parts):
        covar = product(split(state_buf[s]), anom, NT)
        covar = (covar.reshape(levels, EDGE, -1) * rho[None]).reshape(levels * EDGE, -1)
        deltas.append(product(split(covar), weight, NN))
    stores = []
    for s, c in enumerate(starts):
        for l in range(levels):
            loads[s * levels + l][0].wait()
        total_buf[s] += deltas[s]
        for l in range(levels):
            stores.append(
                pltpu.make_async_copy(total_buf.at[s, pl.ds(l * EDGE, EDGE)], out_ref.at[l, pl.ds(c, EDGE)], out_sem.at[s, l])
            )
            stores[-1].start()
    for store in stores:
        store.wait()


def on_device(state_anom, obs_anom, obs_weight, obs_cell, sector_of):
    f32 = jnp.float32
    regions, owners = lax.axis_size("region"), lax.axis_size("state")
    levels, columns, members = state_anom.shape[1:]
    count = obs_anom.shape[1]
    blocks = owners

    slot = jax.ShapeDtypeStruct((SUB, 2 * (CAP // SUB) * members + LANES), f32)
    own_pack, sides, *slots = pl.pallas_call(
        pack_kernel,
        out_shape=[jax.ShapeDtypeStruct((SUB, 2 * (count // SUB) * members + LANES), f32)]
        + [jax.ShapeDtypeStruct((2, SUB, LANES), jnp.int32)]
        + [slot] * (regions - 1),
        in_specs=[HBM] * 4,
        out_specs=[VMEM] * (regions + 1),
        scratch_shapes=[
            pltpu.SMEM((regions,), jnp.int32),
            pltpu.VMEM((count, members), f32),
            pltpu.VMEM((count, members), f32),
            pltpu.VMEM((1, count), jnp.int32),
            pltpu.SemaphoreType.DMA((4,)),
        ],
        compiler_params=limit(8),
        name="pack",
    )(*in_hbm(sector_of, obs_anom, obs_weight, obs_cell))
    got = [exchange(slots[k - 1], "region", k) for k in range(1, regions)]
    packs = [own_pack] + [exchange(own_pack, "state", k) for k in range(1, owners)]
    halo = pl.pallas_call(
        pick_kernel,
        out_shape=jax.ShapeDtypeStruct((SUB, 2 * slot.shape[1]), f32),
        in_specs=[VMEM] * regions,
        out_specs=VMEM,
        compiler_params=limit(4),
        name="pick",
    )(sides, *got)
    halos = [halo] + [exchange(halo, "state", k) for k in range(1, owners)]

    obs = blocks * count
    state = state_anom[0]
    bf16 = jnp.bfloat16
    total = pl.pallas_call(
        functools.partial(own_kernel, blocks),
        out_shape=jax.ShapeDtypeStruct(state.shape, f32),
        in_specs=[HBM] + [VMEM] * blocks,
        out_specs=HBM,
        scratch_shapes=[pltpu.VMEM(state.shape, f32)] * 2
        + [pltpu.VMEM((obs, members), bf16)] * 4
        + [pltpu.VMEM((columns, obs), f32)]
        + [pltpu.SemaphoreType.DMA((levels,))] * 2,
        cost_estimate=pl.CostEstimate(
            flops=12 * levels * columns * obs * members, bytes_accessed=8 * state.size + 8 * obs * members, transcendentals=0
        ),
        compiler_params=limit(24),
        name="own",
    )(*in_hbm(state), *packs)
    out = pl.pallas_call(
        functools.partial(halo_kernel, blocks),
        out_shape=jax.ShapeDtypeStruct(state.shape, f32),
        in_specs=[HBM, HBM] + [VMEM] * blocks,
        out_specs=HBM,
        scratch_shapes=[pltpu.VMEM((2, levels * EDGE, members), f32)] * 2 + [pltpu.SemaphoreType.DMA((2, levels))] * 3,
        input_output_aliases={0: 0},
        compiler_params=limit(16),
        name="halo",
    )(total, *in_hbm(state), *halos)
    return out[None]


def solution(mesh):
    in_specs = (
        P("region", "state", None, None),
        P("region", "state", None),
        P("region", "state", None),
        P("region", "state"),
        P(),
    )
    out_specs = P("region", "state", None, None)
    return jax.shard_map(on_device, mesh=mesh, in_specs=in_specs, out_specs=out_specs, check_vma=False)
```

profile of v0, /device:TPU:0, one launch (start us, length us, event | category | flops | bytes accessed | tf_op | source)
XLA Modules:
  0.0 42.2 jit_solution(16030217821870077105)
XLA Ops:
  0.0 1.1 %pack.1 = (f32[8,8320]{1,0:T(8,128)S(1)}, s32[2,8,128]{2,1,0:T(8,128)S(1)}, f32[8,2176]{1,0:T(8,128)S(1)}, f32[8,2176]{1,0:T(8,128)S(1)}, f32[8,2176]{1,0:T(8,12...) custom-call(s32[8]{0:T(128)} %sector_hbm.1, ...), custom_call_target="tpu_custom_call" | custom-call | tf_op jit(solution)/shard_map/pack/pallas_call | solution.py:237
  1.1 0.6 %collective-permute-start.3 = (f32[8,2176]{1,0:T(8,128)S(1)}, f32[8,2176]{1,0:T(8,128)S(1)}, u32[]{:S(2)}, u32[]{:S(2)}) collective-permute-start(f32[8,2176]{1,0:T(8,128)S(1)} %get-tuple-element.16), channel_id=1, source_target_pairs={{0,4},{4,0},{8,12},{12,8},{16,20},{20,16},{24,28},{28,24},{1,5},{5... | collective-permute-start | bytes 208904 | tf_op jit(solution)/shard_map/ppermute | solution.py:41
  1.6 3.5 %collective-permute-start.2 = (f32[8,8320]{1,0:T(8,128)S(1)}, f32[8,8320]{1,0:T(8,128)S(1)}, u32[]{:S(2)}, u32[]{:S(2)}) collective-permute-start(f32[8,8320]{1,0:T(8,128)S(1)} %get-tuple-element.14.refs_0_), channel_id=1, source_target_pairs={{0,3},{1,2},{2,1},{3,0},{4,7},{5,6},{6,5},{7,4},{8,11},{9,10},{10,... | collective-permute-start | bytes 798728 | tf_op jit(solution)/shard_map/ppermute | solution.py:41
  5.1 0.5 %collective-permute-start.1 = (f32[8,8320]{1,0:T(8,128)S(1)}, f32[8,8320]{1,0:T(8,128)S(1)}, u32[]{:S(2)}, u32[]{:S(2)}) collective-permute-start(f32[8,8320]{1,0:T(8,128)S(1)} %get-tuple-element.14.refs_0_), channel_id=1, source_target_pairs={{0,2},{1,3},{2,0},{3,1},{4,6},{5,7},{6,4},{7,5},{8,10},{9,11},{10,... | collective-permute-start | bytes 798728 | tf_op jit(solution)/shard_map/ppermute | solution.py:41
  5.6 0.1 collective-permute-start
  5.8 2.0 %collective-permute-start.4 = (f32[8,2176]{1,0:T(8,128)S(1)}, f32[8,2176]{1,0:T(8,128)S(1)}, u32[]{:S(2)}, u32[]{:S(2)}) collective-permute-start(f32[8,2176]{1,0:T(8,128)S(1)} %get-tuple-element.17), channel_id=1, source_target_pairs={{0,8},{4,12},{8,0},{12,4},{16,24},{20,28},{24,16},{28,20},{1,9},{5... | collective-permute-start | bytes 208904 | tf_op jit(solution)/shard_map/ppermute | solution.py:41
  7.8 0.0 collective-permute-done.3.refs_0_
  7.8 0.0 collective-permute-start.5
  7.8 2.3 %collective-permute-done.4.refs_1_ = f32[8,2176]{1,0:T(8,128)S(1)} collective-permute-done((f32[8,2176]{1,0:T(8,128)S(1)}, f32[8,2176]{1,0:T(8,128)S(1)}, u32[]{:S(2)}, u32[]{:S(2)}) %collective-permute-start.4) | collective-permute-done | bytes 69664 | tf_op jit(solution)/shard_map/ppermute | solution.py:41
  10.1 3.0 %collective-permute-start.6 = (f32[8,2176]{1,0:T(8,128)S(1)}, f32[8,2176]{1,0:T(8,128)S(1)}, u32[]{:S(2)}, u32[]{:S(2)}) collective-permute-start(f32[8,2176]{1,0:T(8,128)S(1)} %get-tuple-element.19), channel_id=1, source_target_pairs={{0,16},{4,20},{8,24},{12,28},{16,0},{20,4},{24,8},{28,12},{1,17},{... | collective-permute-start | bytes 208904 | tf_op jit(solution)/shard_map/ppermute | solution.py:41
  13.1 0.9 %collective-permute-start.7 = (f32[8,2176]{1,0:T(8,128)S(1)}, f32[8,2176]{1,0:T(8,128)S(1)}, u32[]{:S(2)}, u32[]{:S(2)}) collective-permute-start(f32[8,2176]{1,0:T(8,128)S(1)} %get-tuple-element.20), channel_id=1, source_target_pairs={{0,20},{4,16},{8,28},{12,24},{16,4},{20,0},{24,12},{28,8},{1,21},{... | collective-permute-start | bytes 208904 | tf_op jit(solution)/shard_map/ppermute | solution.py:41
  14.0 1.5 %collective-permute-done.6.refs_3_ = f32[8,2176]{1,0:T(8,128)S(1)} collective-permute-done((f32[8,2176]{1,0:T(8,128)S(1)}, f32[8,2176]{1,0:T(8,128)S(1)}, u32[]{:S(2)}, u32[]{:S(2)}) %collective-permute-start.6) | collective-permute-done | bytes 69664 | tf_op jit(solution)/shard_map/ppermute | solution.py:41
  15.5 6.7 %collective-permute-start.8 = (f32[8,2176]{1,0:T(8,128)S(1)}, f32[8,2176]{1,0:T(8,128)S(1)}, u32[]{:S(2)}, u32[]{:S(2)}) collective-permute-start(f32[8,2176]{1,0:T(8,128)S(1)} %get-tuple-element.21), channel_id=1, source_target_pairs={{0,24},{4,28},{8,16},{12,20},{16,8},{20,12},{24,0},{28,4},{1,25},{... | collective-permute-start | bytes 208904 | tf_op jit(solution)/shard_map/ppermute | solution.py:41
  22.2 0.0 collective-permute-done.7.refs_4_
  22.2 1.6 %collective-permute-start.9 = (f32[8,2176]{1,0:T(8,128)S(1)}, f32[8,2176]{1,0:T(8,128)S(1)}, u32[]{:S(2)}, u32[]{:S(2)}) collective-permute-start(f32[8,2176]{1,0:T(8,128)S(1)} %get-tuple-element.22), channel_id=1, source_target_pairs={{0,28},{4,24},{8,20},{12,16},{16,12},{20,8},{24,4},{28,0},{1,29},{... | collective-permute-start | bytes 208904 | tf_op jit(solution)/shard_map/ppermute | solution.py:41
  23.8 0.8 %collective-permute-done.8.refs_5_ = f32[8,2176]{1,0:T(8,128)S(1)} collective-permute-done((f32[8,2176]{1,0:T(8,128)S(1)}, f32[8,2176]{1,0:T(8,128)S(1)}, u32[]{:S(2)}, u32[]{:S(2)}) %collective-permute-start.8) | collective-permute-done | bytes 69664 | tf_op jit(solution)/shard_map/ppermute | solution.py:41
  24.6 3.1 %collective-permute-done.9.refs_6_ = f32[8,2176]{1,0:T(8,128)S(1)} collective-permute-done((f32[8,2176]{1,0:T(8,128)S(1)}, f32[8,2176]{1,0:T(8,128)S(1)}, u32[]{:S(2)}, u32[]{:S(2)}) %collective-permute-start.9) | collective-permute-done | bytes 69664 | tf_op jit(solution)/shard_map/ppermute | solution.py:41
  27.8 0.1 pick.1.refs_0_
  27.8 2.5 %collective-permute-start.12 = (f32[8,4352]{1,0:T(8,128)S(1)}, f32[8,4352]{1,0:T(8,128)S(1)}, u32[]{:S(2)}, u32[]{:S(2)}) collective-permute-start(f32[8,4352]{1,0:T(8,128)S(1)} %pick.1.refs_0_), channel_id=1, source_target_pairs={{0,3},{1,2},{2,1},{3,0},{4,7},{5,6},{6,5},{7,4},{8,11},{9,10},{10,... | collective-permute-start | bytes 417800 | tf_op jit(solution)/shard_map/ppermute | solution.py:41
  30.3 0.5 %collective-permute-start.11 = (f32[8,4352]{1,0:T(8,128)S(1)}, f32[8,4352]{1,0:T(8,128)S(1)}, u32[]{:S(2)}, u32[]{:S(2)}) collective-permute-start(f32[8,4352]{1,0:T(8,128)S(1)} %pick.1.refs_0_), channel_id=1, source_target_pairs={{0,2},{1,3},{2,0},{3,1},{4,6},{5,7},{6,4},{7,5},{8,10},{9,11},{10,... | collective-permute-start | bytes 417800 | tf_op jit(solution)/shard_map/ppermute | solution.py:41
  30.8 0.0 collective-permute-done.2.refs_3_
  30.8 0.6 %collective-permute-start.10 = (f32[8,4352]{1,0:T(8,128)S(1)}, f32[8,4352]{1,0:T(8,128)S(1)}, u32[]{:S(2)}, u32[]{:S(2)}) collective-permute-start(f32[8,4352]{1,0:T(8,128)S(1)} %pick.1.refs_0_), channel_id=1, source_target_pairs={{0,1},{1,0},{2,3},{3,2},{4,5},{5,4},{6,7},{7,6},{8,9},{9,8},{10,11... | collective-permute-start | bytes 417800 | tf_op jit(solution)/shard_map/ppermute | solution.py:41
  31.4 6.1 %own.1.total_ref = f32[4,256,512]{2,1,0:T(8,128)} custom-call(f32[4,256,512]{2,1,0:T(8,128)} %bitcast.2, f32[8,8320]{1,0:T(8,128)S(1)} %get-tuple-element.14.refs_0_, f32[8,8320]{1,0:T(8,128)S(1)} %collective-permute-done.refs_1_, f32[8,8320]{1,0:T(8,128)S(1)} %collective-permute-done.1.refs_2_, f32[8,8320]{1,0:T(8,128)S(1)} %collective-permute-done.2.refs_3_), custom_call_target="tpu_custom_call" | custom-call | flops 1610612736 | bytes 5242880 | tf_op jit(solution)/shard_map/own/pallas_call | solution.py:269
  37.5 4.6 %halo.1 = f32[4,256,512]{2,1,0:T(8,128)} custom-call(f32[4,256,512]{2,1,0:T(8,128)} %own.1.total_ref, f32[4,256,512]{2,1,0:T(8,128)} %bitcast.3, f32[8,4352]{1,0:T(8,128)S(1)} %pick.1.refs_0_, f32[8,4352]{1,0:T(8,128)S(1)} %collective-permute-done.10.refs_1_, f32[8,4352]{1,0:T(8,128)S(1)} %collective-permute-done.11.refs_2_, ...), custom_call_target="tpu_custom_call", output_to_operand_aliasing={{}: (0, {})} | custom-call | tf_op jit(solution)/shard_map/halo/pallas_call | solution.py:284
  (6 shorter events, 0.0 us)
Async XLA Ops:
  1.1 6.7 %collective-permute-start.3 = (f32[8,2176]{1,0:T(8,128)S(1)}, f32[8,2176]{1,0:T(8,128)S(1)}, u32[]{:S(2)}, u32[]{:S(2)}) collective-permute-start(f32[8,2176]{1,0:T(8,128)S(1)} %get-tuple-element.16), channel_id=1, source_target_pairs={{0,4},{4,0},{8,12},{12,8},{16,20},{20,16},{24,28},{28,24},{1,5},{5... | collective-permute-start | bytes 208904 | tf_op jit(solution)/shard_map/ppermute | solution.py:41
  1.6 29.2 %collective-permute-start.2 = (f32[8,8320]{1,0:T(8,128)S(1)}, f32[8,8320]{1,0:T(8,128)S(1)}, u32[]{:S(2)}, u32[]{:S(2)}) collective-permute-start(f32[8,8320]{1,0:T(8,128)S(1)} %get-tuple-element.14.refs_0_), channel_id=1, source_target_pairs={{0,3},{1,2},{2,1},{3,0},{4,7},{5,6},{6,5},{7,4},{8,11},{9,10},{10,... | collective-permute-start | bytes 798728 | tf_op jit(solution)/shard_map/ppermute | solution.py:41
  5.1 26.3 %collective-permute-start.1 = (f32[8,8320]{1,0:T(8,128)S(1)}, f32[8,8320]{1,0:T(8,128)S(1)}, u32[]{:S(2)}, u32[]{:S(2)}) collective-permute-start(f32[8,8320]{1,0:T(8,128)S(1)} %get-tuple-element.14.refs_0_), channel_id=1, source_target_pairs={{0,2},{1,3},{2,0},{3,1},{4,6},{5,7},{6,4},{7,5},{8,10},{9,11},{10,... | collective-permute-start | bytes 798728 | tf_op jit(solution)/shard_map/ppermute | solution.py:41
  5.6 25.8 %collective-permute-start = (f32[8,8320]{1,0:T(8,128)S(1)}, f32[8,8320]{1,0:T(8,128)S(1)}, u32[]{:S(2)}, u32[]{:S(2)}) collective-permute-start(f32[8,8320]{1,0:T(8,128)S(1)} %get-tuple-element.14.refs_0_), channel_id=1, source_target_pairs={{0,1},{1,0},{2,3},{3,2},{4,5},{5,4},{6,7},{7,6},{8,9},{9,8},{10,11... | collective-permute-start | bytes 798728 | tf_op jit(solution)/shard_map/ppermute | solution.py:41
  5.8 4.3 %collective-permute-start.4 = (f32[8,2176]{1,0:T(8,128)S(1)}, f32[8,2176]{1,0:T(8,128)S(1)}, u32[]{:S(2)}, u32[]{:S(2)}) collective-permute-start(f32[8,2176]{1,0:T(8,128)S(1)} %get-tuple-element.17), channel_id=1, source_target_pairs={{0,8},{4,12},{8,0},{12,4},{16,24},{20,28},{24,16},{28,20},{1,9},{5... | collective-permute-start | bytes 208904 | tf_op jit(solution)/shard_map/ppermute | solution.py:41
  7.8 5.3 %collective-permute-start.5 = (f32[8,2176]{1,0:T(8,128)S(1)}, f32[8,2176]{1,0:T(8,128)S(1)}, u32[]{:S(2)}, u32[]{:S(2)}) collective-permute-start(f32[8,2176]{1,0:T(8,128)S(1)} %get-tuple-element.18), channel_id=1, source_target_pairs={{0,12},{4,8},{8,4},{12,0},{16,28},{20,24},{24,20},{28,16},{1,13},{... | collective-permute-start | bytes 208904 | tf_op jit(solution)/shard_map/ppermute | solution.py:41
  10.1 5.4 %collective-permute-start.6 = (f32[8,2176]{1,0:T(8,128)S(1)}, f32[8,2176]{1,0:T(8,128)S(1)}, u32[]{:S(2)}, u32[]{:S(2)}) collective-permute-start(f32[8,2176]{1,0:T(8,128)S(1)} %get-tuple-element.19), channel_id=1, source_target_pairs={{0,16},{4,20},{8,24},{12,28},{16,0},{20,4},{24,8},{28,12},{1,17},{... | collective-permute-start | bytes 208904 | tf_op jit(solution)/shard_map/ppermute | solution.py:41
  13.1 9.2 %collective-permute-start.7 = (f32[8,2176]{1,0:T(8,128)S(1)}, f32[8,2176]{1,0:T(8,128)S(1)}, u32[]{:S(2)}, u32[]{:S(2)}) collective-permute-start(f32[8,2176]{1,0:T(8,128)S(1)} %get-tuple-element.20), channel_id=1, source_target_pairs={{0,20},{4,16},{8,28},{12,24},{16,4},{20,0},{24,12},{28,8},{1,21},{... | collective-permute-start | bytes 208904 | tf_op jit(solution)/shard_map/ppermute | solution.py:41
  15.5 9.1 %collective-permute-start.8 = (f32[8,2176]{1,0:T(8,128)S(1)}, f32[8,2176]{1,0:T(8,128)S(1)}, u32[]{:S(2)}, u32[]{:S(2)}) collective-permute-start(f32[8,2176]{1,0:T(8,128)S(1)} %get-tuple-element.21), channel_id=1, source_target_pairs={{0,24},{4,28},{8,16},{12,20},{16,8},{20,12},{24,0},{28,4},{1,25},{... | collective-permute-start | bytes 208904 | tf_op jit(solution)/shard_map/ppermute | solution.py:41
  22.2 5.5 %collective-permute-start.9 = (f32[8,2176]{1,0:T(8,128)S(1)}, f32[8,2176]{1,0:T(8,128)S(1)}, u32[]{:S(2)}, u32[]{:S(2)}) collective-permute-start(f32[8,2176]{1,0:T(8,128)S(1)} %get-tuple-element.22), channel_id=1, source_target_pairs={{0,28},{4,24},{8,20},{12,16},{16,12},{20,8},{24,4},{28,0},{1,29},{... | collective-permute-start | bytes 208904 | tf_op jit(solution)/shard_map/ppermute | solution.py:41
  27.8 9.7 %collective-permute-start.12 = (f32[8,4352]{1,0:T(8,128)S(1)}, f32[8,4352]{1,0:T(8,128)S(1)}, u32[]{:S(2)}, u32[]{:S(2)}) collective-permute-start(f32[8,4352]{1,0:T(8,128)S(1)} %pick.1.refs_0_), channel_id=1, source_target_pairs={{0,3},{1,2},{2,1},{3,0},{4,7},{5,6},{6,5},{7,4},{8,11},{9,10},{10,... | collective-permute-start | bytes 417800 | tf_op jit(solution)/shard_map/ppermute | solution.py:41
  30.3 7.2 %collective-permute-start.11 = (f32[8,4352]{1,0:T(8,128)S(1)}, f32[8,4352]{1,0:T(8,128)S(1)}, u32[]{:S(2)}, u32[]{:S(2)}) collective-permute-start(f32[8,4352]{1,0:T(8,128)S(1)} %pick.1.refs_0_), channel_id=1, source_target_pairs={{0,2},{1,3},{2,0},{3,1},{4,6},{5,7},{6,4},{7,5},{8,10},{9,11},{10,... | collective-permute-start | bytes 417800 | tf_op jit(solution)/shard_map/ppermute | solution.py:41
  30.8 6.7 %collective-permute-start.10 = (f32[8,4352]{1,0:T(8,128)S(1)}, f32[8,4352]{1,0:T(8,128)S(1)}, u32[]{:S(2)}, u32[]{:S(2)}) collective-permute-start(f32[8,4352]{1,0:T(8,128)S(1)} %pick.1.refs_0_), channel_id=1, source_target_pairs={{0,1},{1,0},{2,3},{3,2},{4,5},{5,4},{6,7},{7,6},{8,9},{9,8},{10,11... | collective-permute-start | bytes 417800 | tf_op jit(solution)/shard_map/ppermute | solution.py:41
where the time goes:
time: 42.4 us; the launch traced here: 42.2 us
  starting transfers between devices  22.5 us (53%)
  Pallas kernels  11.9 us (28%)
  waiting for transfers between devices  7.75 us (18%)
    ppermute x13, starting transfers between devices, exchange(): lax.ppermute(value, axis, [(i, target(i, step, size)) for i in range(size)])  22.5 us
    ppermute x13, waiting for transfers between devices, exchange(): lax.ppermute(value, axis, [(i, target(i, step, size)) for i in range(size)])  7.75 us
    pallas_call x1, Pallas kernels, on_device(): pl.pallas_call(functools.partial(own_kernel, blocks), out_shape=jax.Shape...  6.09 us
    pallas_call x1, Pallas kernels, on_device(): pl.pallas_call(functools.partial(halo_kernel, blocks), out_shape=jax.Shap...  4.65 us
    pallas_call x1, Pallas kernels, on_device(): pl.pallas_call(pack_kernel, out_shape=[jax.ShapeDtypeStruct((SUB, 2 * (co...  1.07 us
  transfers between devices with their start and end apart: 13, of which 4 were waited for; matrix products, arithmetic and copies ran while one was open for 0% of the time, Pallas kernels for 15%

commit v1 on v0

--- a/solution.py
+++ b/solution.py
@@ -141,8 +141,16 @@
             halo_ref[:, side * width + at : side * width + at + LANES] = value
 
 
+def joined(left, right, dims):
+    axis = dims[1][0]
+    lefts = jnp.concatenate([left[0], left[0], left[1]], axis=1)
+    rights = jnp.concatenate([right[0], right[1], right[0]], axis=axis)
+    return lax.dot_general(lefts, rights, (dims, ((), ())), preferred_element_type=jnp.float32)
+
+
 def own_kernel(blocks, state_hbm, *refs):
-    pack_refs, (out_hbm, state_ref, out_ref, a_hi, a_lo, w_hi, w_lo, rho_ref, in_sem, out_sem) = refs[:blocks], refs[blocks:]
+    pack_refs, (out_hbm, edge_ref, s_hi, s_lo) = refs[:blocks], refs[blocks : blocks + 4]
+    state_ref, out_ref, a_hi, a_lo, w_hi, w_lo, rho_ref, in_sem, out_sem = refs[blocks + 4 :]
     levels, rows, members = state_ref.shape
     half = pack_refs[0].shape[1] // 2 // LANES * LANES
     count = half // members * SUB
@@ -164,34 +172,30 @@
     stores = []
     for l in range(levels):
         loads[l].wait()
-        covar = product(split(state_ref[l]), (a_hi[...], a_lo[...]), NT) * rho_ref[...]
-        out_ref[l] = product(split(covar), (w_hi[...], w_lo[...]), NN)
-        stores.append(pltpu.make_async_copy(out_ref.at[l], out_hbm.at[l], out_sem.at[l]))
+        high, low = split(state_ref[l])
+        covar = product((high, low), (a_hi[...], a_lo[...]), NT) * rho_ref[...]
+        total = product(split(covar), (w_hi[...], w_lo[...]), NN)
+        out_ref[l] = total[EDGE : rows - EDGE]
+        stores.append(pltpu.make_async_copy(out_ref.at[l], out_hbm.at[l, pl.ds(EDGE, rows - 2 * EDGE)], out_sem.at[l]))
         stores[-1].start()
+        here = pl.ds(l * EDGE, EDGE)
+        for side, part in enumerate((slice(0, EDGE), slice(rows - EDGE, rows))):
+            edge_ref[side, here, :] = total[part]
+            s_hi[side, here, :] = high[part]
+            s_lo[side, here, :] = low[part]
     for store in stores:
         store.wait()
 
 
-def halo_kernel(blocks, total_ref, state_ref, *refs):
-    halo_refs, (out_ref, total_buf, state_buf, in_sem, state_sem, out_sem) = refs[:blocks], refs[blocks:]
-    levels, columns, members = state_ref.shape
+def halo_kernel(blocks, total_hbm, edge_ref, s_hi, s_lo, *refs):
+    halo_refs, (out_hbm, out_ref, out_sem) = refs[:blocks], refs[blocks:]
+    levels, columns, members = out_hbm.shape
     wide = CAP // SUB * members
     width = halo_refs[0].shape[1] // 2
     starts = (0, columns - EDGE)
-    loads = [
-        (
-            pltpu.make_async_copy(total_ref.at[l, pl.ds(c, EDGE)], total_buf.at[s, pl.ds(l * EDGE, EDGE)], in_sem.at[s, l]),
-            pltpu.make_async_copy(state_ref.at[l, pl.ds(c, EDGE)], state_buf.at[s, pl.ds(l * EDGE, EDGE)], state_sem.at[s, l]),
-        )
-        for s, c in enumerate(starts)
-        for l in range(levels)
-    ]
-    for total_load, state_load in loads:
-        state_load.start()
-        total_load.start()
     lane = lax.broadcasted_iota(jnp.int32, (1, LANES), 1)
     per = LANES // CAP
-    parts = []
+    stores = []
     for s, shift in enumerate((-SECT_W, SECT_W)):
         at = s * width
         anom = split(jnp.concatenate([unfolded(h[:, at : at + wide], members) for h in halo_refs], axis=0))
@@ -204,24 +208,16 @@
                 cells = jnp.where(lane >= b * CAP, tiles[g + b], cells)
             groups.append(cells)
         cells = jnp.concatenate(groups, axis=1)[:, : blocks * CAP]
-        parts.append((anom, weight, taper(starts[s], EDGE, cells, shift) / (members - 1)))
-    for _, state_load in loads:
-        state_load.wait()
-    deltas = []
-    for s, (anom, weight, rho) in enumerate(parts):
-        covar = product(split(state_buf[s]), anom, NT)
+        rho = taper(starts[s], EDGE, cells, shift) / (members - 1)
+        covar = product((s_hi[s], s_lo[s]), anom, NT)
         covar = (covar.reshape(levels, EDGE, -1) * rho[None]).reshape(levels * EDGE, -1)
-        deltas.append(product(split(covar), weight, NN))
-    stores = []
-    for s, c in enumerate(starts):
+        out_ref[s] = edge_ref[s] + joined(split(covar), weight, NN)
         for l in range(levels):
-            loads[s * levels + l][0].wait()
-        total_buf[s] += deltas[s]
-        for l in range(levels):
-            stores.append(
-                pltpu.make_async_copy(total_buf.at[s, pl.ds(l * EDGE, EDGE)], out_ref.at[l, pl.ds(c, EDGE)], out_sem.at[s, l])
+            store = pltpu.make_async_copy(
+                out_ref.at[s, pl.ds(l * EDGE, EDGE)], out_hbm.at[l, pl.ds(starts[s], EDGE)], out_sem.at[s, l]
             )
-            stores[-1].start()
+            store.start()
+            stores.append(store)
     for store in stores:
         store.wait()
 
@@ -266,12 +262,15 @@
     obs = blocks * count
     state = state_anom[0]
     bf16 = jnp.bfloat16
-    total = pl.pallas_call(
+    middle = columns - 2 * EDGE
+    edges = (2, levels * EDGE, members)
+    total, *kept = pl.pallas_call(
         functools.partial(own_kernel, blocks),
-        out_shape=jax.ShapeDtypeStruct(state.shape, f32),
+        out_shape=[jax.ShapeDtypeStruct(state.shape, f32), jax.ShapeDtypeStruct(edges, f32)]
+        + [jax.ShapeDtypeStruct(edges, bf16)] * 2,
         in_specs=[HBM] + [VMEM] * blocks,
-        out_specs=HBM,
-        scratch_shapes=[pltpu.VMEM(state.shape, f32)] * 2
+        out_specs=[HBM] + [VMEM] * 3,
+        scratch_shapes=[pltpu.VMEM(state.shape, f32), pltpu.VMEM((levels, middle, members), f32)]
         + [pltpu.VMEM((obs, members), bf16)] * 4
         + [pltpu.VMEM((columns, obs), f32)]
         + [pltpu.SemaphoreType.DMA((levels,))] * 2,
@@ -284,13 +283,13 @@
     out = pl.pallas_call(
         functools.partial(halo_kernel, blocks),
         out_shape=jax.ShapeDtypeStruct(state.shape, f32),
-        in_specs=[HBM, HBM] + [VMEM] * blocks,
+        in_specs=[HBM] + [VMEM] * (3 + blocks),
         out_specs=HBM,
-        scratch_shapes=[pltpu.VMEM((2, levels * EDGE, members), f32)] * 2 + [pltpu.SemaphoreType.DMA((2, levels))] * 3,
+        scratch_shapes=[pltpu.VMEM(edges, f32), pltpu.SemaphoreType.DMA((2, levels))],
         input_output_aliases={0: 0},
         compiler_params=limit(16),
         name="halo",
-    )(total, *in_hbm(state), *halos)
+    )(total, *kept, *halos)
     return out[None]
 
 

time: 42.4 us -> 39.9 us (0.941)
  Pallas kernels: 11.9 us -> 9.43 us
    pallas_call x1, Pallas kernels: 4.65 us -> 2.32 us  [on_device(): pl.pallas_call(functools.partial(halo_kernel, blocks), out_shape=jax.Shap...]
where the time goes in v1:
time: 39.9 us; the launch traced here: 39.7 us
  starting transfers between devices  22.5 us (56%)
  Pallas kernels  9.43 us (24%)
  waiting for transfers between devices  7.75 us (19%)
    ppermute x13, starting transfers between devices, exchange(): lax.ppermute(value, axis, [(i, target(i, step, size)) for i in range(size)])  22.5 us
    ppermute x13, waiting for transfers between devices, exchange(): lax.ppermute(value, axis, [(i, target(i, step, size)) for i in range(size)])  7.75 us
    pallas_call x1, Pallas kernels, on_device(): pl.pallas_call(functools.partial(own_kernel, blocks), out_shape=[jax.Shap...  5.99 us
    pallas_call x1, Pallas kernels, on_device(): pl.pallas_call(functools.partial(halo_kernel, blocks), out_shape=jax.Shap...  2.32 us
    pallas_call x1, Pallas kernels, on_device(): pl.pallas_call(pack_kernel, out_shape=[jax.ShapeDtypeStruct((SUB, 2 * (co...  1.07 us
  transfers between devices with their start and end apart: 13, of which 4 were waited for; matrix products, arithmetic and copies ran while one was open for 0% of the time, Pallas kernels for 15%

profile of v1, /device:TPU:0, one launch (start us, length us, event | category | flops | bytes accessed | tf_op | source)
XLA Modules:
  0.0 39.7 jit_solution(13495256156011558307)
XLA Ops:
  0.0 1.1 %pack.1 = (f32[8,8320]{1,0:T(8,128)S(1)}, s32[2,8,128]{2,1,0:T(8,128)S(1)}, f32[8,2176]{1,0:T(8,128)S(1)}, f32[8,2176]{1,0:T(8,128)S(1)}, f32[8,2176]{1,0:T(8,12...) custom-call(s32[8]{0:T(128)} %sector_hbm.1, ...), custom_call_target="tpu_custom_call" | custom-call | tf_op jit(solution)/shard_map/pack/pallas_call | solution.py:233
  1.1 0.6 %collective-permute-start.3 = (f32[8,2176]{1,0:T(8,128)S(1)}, f32[8,2176]{1,0:T(8,128)S(1)}, u32[]{:S(2)}, u32[]{:S(2)}) collective-permute-start(f32[8,2176]{1,0:T(8,128)S(1)} %get-tuple-element.24), channel_id=1, source_target_pairs={{0,4},{4,0},{8,12},{12,8},{16,20},{20,16},{24,28},{28,24},{1,5},{5... | collective-permute-start | bytes 208904 | tf_op jit(solution)/shard_map/ppermute | solution.py:41
  1.6 3.5 %collective-permute-start.2 = (f32[8,8320]{1,0:T(8,128)S(1)}, f32[8,8320]{1,0:T(8,128)S(1)}, u32[]{:S(2)}, u32[]{:S(2)}) collective-permute-start(f32[8,8320]{1,0:T(8,128)S(1)} %get-tuple-element.18.refs_0_), channel_id=1, source_target_pairs={{0,3},{1,2},{2,1},{3,0},{4,7},{5,6},{6,5},{7,4},{8,11},{9,10},{10,... | collective-permute-start | bytes 798728 | tf_op jit(solution)/shard_map/ppermute | solution.py:41
  5.1 0.5 %collective-permute-start.1 = (f32[8,8320]{1,0:T(8,128)S(1)}, f32[8,8320]{1,0:T(8,128)S(1)}, u32[]{:S(2)}, u32[]{:S(2)}) collective-permute-start(f32[8,8320]{1,0:T(8,128)S(1)} %get-tuple-element.18.refs_0_), channel_id=1, source_target_pairs={{0,2},{1,3},{2,0},{3,1},{4,6},{5,7},{6,4},{7,5},{8,10},{9,11},{10,... | collective-permute-start | bytes 798728 | tf_op jit(solution)/shard_map/ppermute | solution.py:41
  5.6 0.1 collective-permute-start
  5.8 2.0 %collective-permute-start.4 = (f32[8,2176]{1,0:T(8,128)S(1)}, f32[8,2176]{1,0:T(8,128)S(1)}, u32[]{:S(2)}, u32[]{:S(2)}) collective-permute-start(f32[8,2176]{1,0:T(8,128)S(1)} %get-tuple-element.25), channel_id=1, source_target_pairs={{0,8},{4,12},{8,0},{12,4},{16,24},{20,28},{24,16},{28,20},{1,9},{5... | collective-permute-start | bytes 208904 | tf_op jit(solution)/shard_map/ppermute | solution.py:41
  7.8 0.0 collective-permute-done.3.refs_0_
  7.8 0.0 collective-permute-start.5
  7.8 2.3 %collective-permute-done.4.refs_1_ = f32[8,2176]{1,0:T(8,128)S(1)} collective-permute-done((f32[8,2176]{1,0:T(8,128)S(1)}, f32[8,2176]{1,0:T(8,128)S(1)}, u32[]{:S(2)}, u32[]{:S(2)}) %collective-permute-start.4) | collective-permute-done | bytes 69664 | tf_op jit(solution)/shard_map/ppermute | solution.py:41
  10.1 3.0 %collective-permute-start.6 = (f32[8,2176]{1,0:T(8,128)S(1)}, f32[8,2176]{1,0:T(8,128)S(1)}, u32[]{:S(2)}, u32[]{:S(2)}) collective-permute-start(f32[8,2176]{1,0:T(8,128)S(1)} %get-tuple-element.27), channel_id=1, source_target_pairs={{0,16},{4,20},{8,24},{12,28},{16,0},{20,4},{24,8},{28,12},{1,17},{... | collective-permute-start | bytes 208904 | tf_op jit(solution)/shard_map/ppermute | solution.py:41
  13.1 0.9 %collective-permute-start.7 = (f32[8,2176]{1,0:T(8,128)S(1)}, f32[8,2176]{1,0:T(8,128)S(1)}, u32[]{:S(2)}, u32[]{:S(2)}) collective-permute-start(f32[8,2176]{1,0:T(8,128)S(1)} %get-tuple-element.28), channel_id=1, source_target_pairs={{0,20},{4,16},{8,28},{12,24},{16,4},{20,0},{24,12},{28,8},{1,21},{... | collective-permute-start | bytes 208904 | tf_op jit(solution)/shard_map/ppermute | solution.py:41
  14.0 1.5 %collective-permute-done.6.refs_3_ = f32[8,2176]{1,0:T(8,128)S(1)} collective-permute-done((f32[8,2176]{1,0:T(8,128)S(1)}, f32[8,2176]{1,0:T(8,128)S(1)}, u32[]{:S(2)}, u32[]{:S(2)}) %collective-permute-start.6) | collective-permute-done | bytes 69664 | tf_op jit(solution)/shard_map/ppermute | solution.py:41
  15.5 6.7 %collective-permute-start.8 = (f32[8,2176]{1,0:T(8,128)S(1)}, f32[8,2176]{1,0:T(8,128)S(1)}, u32[]{:S(2)}, u32[]{:S(2)}) collective-permute-start(f32[8,2176]{1,0:T(8,128)S(1)} %get-tuple-element.29), channel_id=1, source_target_pairs={{0,24},{4,28},{8,16},{12,20},{16,8},{20,12},{24,0},{28,4},{1,25},{... | collective-permute-start | bytes 208904 | tf_op jit(solution)/shard_map/ppermute | solution.py:41
  22.2 0.0 collective-permute-done.7.refs_4_
  22.2 1.6 %collective-permute-start.9 = (f32[8,2176]{1,0:T(8,128)S(1)}, f32[8,2176]{1,0:T(8,128)S(1)}, u32[]{:S(2)}, u32[]{:S(2)}) collective-permute-start(f32[8,2176]{1,0:T(8,128)S(1)} %get-tuple-element.30), channel_id=1, source_target_pairs={{0,28},{4,24},{8,20},{12,16},{16,12},{20,8},{24,4},{28,0},{1,29},{... | collective-permute-start | bytes 208904 | tf_op jit(solution)/shard_map/ppermute | solution.py:41
  23.8 0.8 %collective-permute-done.8.refs_5_ = f32[8,2176]{1,0:T(8,128)S(1)} collective-permute-done((f32[8,2176]{1,0:T(8,128)S(1)}, f32[8,2176]{1,0:T(8,128)S(1)}, u32[]{:S(2)}, u32[]{:S(2)}) %collective-permute-start.8) | collective-permute-done | bytes 69664 | tf_op jit(solution)/shard_map/ppermute | solution.py:41
  24.6 3.1 %collective-permute-done.9.refs_6_ = f32[8,2176]{1,0:T(8,128)S(1)} collective-permute-done((f32[8,2176]{1,0:T(8,128)S(1)}, f32[8,2176]{1,0:T(8,128)S(1)}, u32[]{:S(2)}, u32[]{:S(2)}) %collective-permute-start.9) | collective-permute-done | bytes 69664 | tf_op jit(solution)/shard_map/ppermute | solution.py:41
  27.8 0.1 pick.1.refs_0_
  27.8 2.5 %collective-permute-start.12 = (f32[8,4352]{1,0:T(8,128)S(1)}, f32[8,4352]{1,0:T(8,128)S(1)}, u32[]{:S(2)}, u32[]{:S(2)}) collective-permute-start(f32[8,4352]{1,0:T(8,128)S(1)} %pick.1.refs_0_), channel_id=1, source_target_pairs={{0,3},{1,2},{2,1},{3,0},{4,7},{5,6},{6,5},{7,4},{8,11},{9,10},{10,... | collective-permute-start | bytes 417800 | tf_op jit(solution)/shard_map/ppermute | solution.py:41
  30.3 0.5 %collective-permute-start.11 = (f32[8,4352]{1,0:T(8,128)S(1)}, f32[8,4352]{1,0:T(8,128)S(1)}, u32[]{:S(2)}, u32[]{:S(2)}) collective-permute-start(f32[8,4352]{1,0:T(8,128)S(1)} %pick.1.refs_0_), channel_id=1, source_target_pairs={{0,2},{1,3},{2,0},{3,1},{4,6},{5,7},{6,4},{7,5},{8,10},{9,11},{10,... | collective-permute-start | bytes 417800 | tf_op jit(solution)/shard_map/ppermute | solution.py:41
  30.8 0.0 collective-permute-done.2.refs_3_
  30.8 0.6 %collective-permute-start.10 = (f32[8,4352]{1,0:T(8,128)S(1)}, f32[8,4352]{1,0:T(8,128)S(1)}, u32[]{:S(2)}, u32[]{:S(2)}) collective-permute-start(f32[8,4352]{1,0:T(8,128)S(1)} %pick.1.refs_0_), channel_id=1, source_target_pairs={{0,1},{1,0},{2,3},{3,2},{4,5},{5,4},{6,7},{7,6},{8,9},{9,8},{10,11... | collective-permute-start | bytes 417800 | tf_op jit(solution)/shard_map/ppermute | solution.py:41
  31.4 6.0 %own.1 = (f32[4,256,512]{2,1,0:T(8,128)}, f32[2,256,512]{2,1,0:T(8,128)S(1)}, bf16[2,256,512]{2,1,0:T(8,128)(2,1)S(1)}, bf16[2,256,512]{2,1,0:T(8,128)(2,1)S(1)}) custom-call(f32[4,256,512]{2,1,0:T(8,128)} %bitcast.2, f32[8,8320]{1,0:T(8,128)S(1)} %get-tuple-element.18.refs_0_, f32[8,8320]{1,0:T(8,128)S(1)} %collective-permute-done.refs_1_, ...), custom_call_target="tpu_custom_call" | custom-call | flops 1610612736 | bytes 5242880 | tf_op jit(solution)/shard_map/own/pallas_call | solution.py:267
  37.4 2.3 %halo.1 = f32[4,256,512]{2,1,0:T(8,128)} custom-call(f32[4,256,512]{2,1,0:T(8,128)} %get-tuple-element.19.total_hbm, f32[2,256,512]{2,1,0:T(8,128)S(1)} %get-tuple-element.20.edge_ref, bf16[2,256,512]{2,1,0:T(8,128)(2,1)S(1)} %get-tuple-element.21.s_hi, bf16[2,256,512]{2,1,0:T(8,128)(2,1)S(1)} %get-tuple-element.22.s_lo, ...), custom_call_target="tpu_custom_call", output_to_operand_aliasing={{}: (0, {})} | custom-call | tf_op jit(solution)/shard_map/halo/pallas_call | solution.py:283
  (6 shorter events, 0.0 us)
Async XLA Ops:
  1.1 6.7 %collective-permute-start.3 = (f32[8,2176]{1,0:T(8,128)S(1)}, f32[8,2176]{1,0:T(8,128)S(1)}, u32[]{:S(2)}, u32[]{:S(2)}) collective-permute-start(f32[8,2176]{1,0:T(8,128)S(1)} %get-tuple-element.24), channel_id=1, source_target_pairs={{0,4},{4,0},{8,12},{12,8},{16,20},{20,16},{24,28},{28,24},{1,5},{5... | collective-permute-start | bytes 208904 | tf_op jit(solution)/shard_map/ppermute | solution.py:41
  1.6 29.2 %collective-permute-start.2 = (f32[8,8320]{1,0:T(8,128)S(1)}, f32[8,8320]{1,0:T(8,128)S(1)}, u32[]{:S(2)}, u32[]{:S(2)}) collective-permute-start(f32[8,8320]{1,0:T(8,128)S(1)} %get-tuple-element.18.refs_0_), channel_id=1, source_target_pairs={{0,3},{1,2},{2,1},{3,0},{4,7},{5,6},{6,5},{7,4},{8,11},{9,10},{10,... | collective-permute-start | bytes 798728 | tf_op jit(solution)/shard_map/ppermute | solution.py:41
  5.1 26.3 %collective-permute-start.1 = (f32[8,8320]{1,0:T(8,128)S(1)}, f32[8,8320]{1,0:T(8,128)S(1)}, u32[]{:S(2)}, u32[]{:S(2)}) collective-permute-start(f32[8,8320]{1,0:T(8,128)S(1)} %get-tuple-element.18.refs_0_), channel_id=1, source_target_pairs={{0,2},{1,3},{2,0},{3,1},{4,6},{5,7},{6,4},{7,5},{8,10},{9,11},{10,... | collective-permute-start | bytes 798728 | tf_op jit(solution)/shard_map/ppermute | solution.py:41
  5.6 25.8 %collective-permute-start = (f32[8,8320]{1,0:T(8,128)S(1)}, f32[8,8320]{1,0:T(8,128)S(1)}, u32[]{:S(2)}, u32[]{:S(2)}) collective-permute-start(f32[8,8320]{1,0:T(8,128)S(1)} %get-tuple-element.18.refs_0_), channel_id=1, source_target_pairs={{0,1},{1,0},{2,3},{3,2},{4,5},{5,4},{6,7},{7,6},{8,9},{9,8},{10,11... | collective-permute-start | bytes 798728 | tf_op jit(solution)/shard_map/ppermute | solution.py:41
  5.8 4.3 %collective-permute-start.4 = (f32[8,2176]{1,0:T(8,128)S(1)}, f32[8,2176]{1,0:T(8,128)S(1)}, u32[]{:S(2)}, u32[]{:S(2)}) collective-permute-start(f32[8,2176]{1,0:T(8,128)S(1)} %get-tuple-element.25), channel_id=1, source_target_pairs={{0,8},{4,12},{8,0},{12,4},{16,24},{20,28},{24,16},{28,20},{1,9},{5... | collective-permute-start | bytes 208904 | tf_op jit(solution)/shard_map/ppermute | solution.py:41
  7.8 5.3 %collective-permute-start.5 = (f32[8,2176]{1,0:T(8,128)S(1)}, f32[8,2176]{1,0:T(8,128)S(1)}, u32[]{:S(2)}, u32[]{:S(2)}) collective-permute-start(f32[8,2176]{1,0:T(8,128)S(1)} %get-tuple-element.26), channel_id=1, source_target_pairs={{0,12},{4,8},{8,4},{12,0},{16,28},{20,24},{24,20},{28,16},{1,13},{... | collective-permute-start | bytes 208904 | tf_op jit(solution)/shard_map/ppermute | solution.py:41
  10.1 5.4 %collective-permute-start.6 = (f32[8,2176]{1,0:T(8,128)S(1)}, f32[8,2176]{1,0:T(8,128)S(1)}, u32[]{:S(2)}, u32[]{:S(2)}) collective-permute-start(f32[8,2176]{1,0:T(8,128)S(1)} %get-tuple-element.27), channel_id=1, source_target_pairs={{0,16},{4,20},{8,24},{12,28},{16,0},{20,4},{24,8},{28,12},{1,17},{... | collective-permute-start | bytes 208904 | tf_op jit(solution)/shard_map/ppermute | solution.py:41
  13.1 9.2 %collective-permute-start.7 = (f32[8,2176]{1,0:T(8,128)S(1)}, f32[8,2176]{1,0:T(8,128)S(1)}, u32[]{:S(2)}, u32[]{:S(2)}) collective-permute-start(f32[8,2176]{1,0:T(8,128)S(1)} %get-tuple-element.28), channel_id=1, source_target_pairs={{0,20},{4,16},{8,28},{12,24},{16,4},{20,0},{24,12},{28,8},{1,21},{... | collective-permute-start | bytes 208904 | tf_op jit(solution)/shard_map/ppermute | solution.py:41
  15.5 9.1 %collective-permute-start.8 = (f32[8,2176]{1,0:T(8,128)S(1)}, f32[8,2176]{1,0:T(8,128)S(1)}, u32[]{:S(2)}, u32[]{:S(2)}) collective-permute-start(f32[8,2176]{1,0:T(8,128)S(1)} %get-tuple-element.29), channel_id=1, source_target_pairs={{0,24},{4,28},{8,16},{12,20},{16,8},{20,12},{24,0},{28,4},{1,25},{... | collective-permute-start | bytes 208904 | tf_op jit(solution)/shard_map/ppermute | solution.py:41
  22.2 5.5 %collective-permute-start.9 = (f32[8,2176]{1,0:T(8,128)S(1)}, f32[8,2176]{1,0:T(8,128)S(1)}, u32[]{:S(2)}, u32[]{:S(2)}) collective-permute-start(f32[8,2176]{1,0:T(8,128)S(1)} %get-tuple-element.30), channel_id=1, source_target_pairs={{0,28},{4,24},{8,20},{12,16},{16,12},{20,8},{24,4},{28,0},{1,29},{... | collective-permute-start | bytes 208904 | tf_op jit(solution)/shard_map/ppermute | solution.py:41
  27.8 9.6 %collective-permute-start.12 = (f32[8,4352]{1,0:T(8,128)S(1)}, f32[8,4352]{1,0:T(8,128)S(1)}, u32[]{:S(2)}, u32[]{:S(2)}) collective-permute-start(f32[8,4352]{1,0:T(8,128)S(1)} %pick.1.refs_0_), channel_id=1, source_target_pairs={{0,3},{1,2},{2,1},{3,0},{4,7},{5,6},{6,5},{7,4},{8,11},{9,10},{10,... | collective-permute-start | bytes 417800 | tf_op jit(solution)/shard_map/ppermute | solution.py:41
  30.3 7.1 %collective-permute-start.11 = (f32[8,4352]{1,0:T(8,128)S(1)}, f32[8,4352]{1,0:T(8,128)S(1)}, u32[]{:S(2)}, u32[]{:S(2)}) collective-permute-start(f32[8,4352]{1,0:T(8,128)S(1)} %pick.1.refs_0_), channel_id=1, source_target_pairs={{0,2},{1,3},{2,0},{3,1},{4,6},{5,7},{6,4},{7,5},{8,10},{9,11},{10,... | collective-permute-start | bytes 417800 | tf_op jit(solution)/shard_map/ppermute | solution.py:41
  30.8 6.6 %collective-permute-start.10 = (f32[8,4352]{1,0:T(8,128)S(1)}, f32[8,4352]{1,0:T(8,128)S(1)}, u32[]{:S(2)}, u32[]{:S(2)}) collective-permute-start(f32[8,4352]{1,0:T(8,128)S(1)} %pick.1.refs_0_), channel_id=1, source_target_pairs={{0,1},{1,0},{2,3},{3,2},{4,5},{5,4},{6,7},{7,6},{8,9},{9,8},{10,11... | collective-permute-start | bytes 417800 | tf_op jit(solution)/shard_map/ppermute | solution.py:41

commit v2 on v1

--- a/solution.py
+++ b/solution.py
@@ -148,41 +148,48 @@
     return lax.dot_general(lefts, rights, (dims, ((), ())), preferred_element_type=jnp.float32)
 
 
-def own_kernel(blocks, state_hbm, *refs):
-    pack_refs, (out_hbm, edge_ref, s_hi, s_lo) = refs[:blocks], refs[blocks : blocks + 4]
-    state_ref, out_ref, a_hi, a_lo, w_hi, w_lo, rho_ref, in_sem, out_sem = refs[blocks + 4 :]
-    levels, rows, members = state_ref.shape
+def prep_kernel(state_hbm, hi_ref, lo_ref, state_ref, sems):
+    levels, rows = state_ref.shape[:2]
+    loads = [pltpu.make_async_copy(state_hbm.at[l], state_ref.at[l], sems.at[l]) for l in range(levels)]
+    for load in loads:
+        load.start()
+    for l in range(levels):
+        loads[l].wait()
+        here = pl.ds(l * rows, rows)
+        hi_ref[here, :], lo_ref[here, :] = split(state_ref[l])
+
+
+def own_kernel(blocks, s_hi, s_lo, *refs):
+    pack_refs, (out_hbm, edge_ref, out_ref, a_hi, a_lo, w_hi, w_lo, out_sem) = refs[:blocks], refs[blocks:]
+    levels, middle, members = out_ref.shape
+    rows = middle + 2 * EDGE
     half = pack_refs[0].shape[1] // 2 // LANES * LANES
     count = half // members * SUB
-    loads = [pltpu.make_async_copy(state_hbm.at[l], state_ref.at[l], in_sem.at[l]) for l in range(levels)]
-    for load in loads:
-        load.start()
     lane = lax.broadcasted_iota(jnp.int32, (1, LANES), 1)
-    tiles = [pack[:1, 2 * half :] for pack in pack_refs]
     for b in range(blocks):
         here = pl.ds(b * count, count)
         a_hi[here, :], a_lo[here, :] = split(unfolded(pack_refs[b][:, :half], members))
+    for b in range(blocks):
+        here = pl.ds(b * count, count)
         w_hi[here, :], w_lo[here, :] = split(unfolded(pack_refs[b][:, half : 2 * half], members))
     each = LANES // count
+    groups = []
     for g in range(0, blocks, each):
-        cells = tiles[g]
+        cells = pack_refs[g][:1, 2 * half :]
         for b in range(1, each):
-            cells = jnp.where(lane >= b * count, tiles[g + b], cells)
-        rho_ref[:, g * count : g * count + LANES] = taper(0, rows, cells, 0) / (members - 1)
+            cells = jnp.where(lane >= b * count, pack_refs[g + b][:1, 2 * half :], cells)
+        groups.append(taper(0, rows, cells, 0) / (members - 1))
+    rho = jnp.concatenate(groups, axis=1)
     stores = []
     for l in range(levels):
-        loads[l].wait()
-        high, low = split(state_ref[l])
-        covar = product((high, low), (a_hi[...], a_lo[...]), NT) * rho_ref[...]
+        here = pl.ds(l * rows, rows)
+        covar = product((s_hi[here, :], s_lo[here, :]), (a_hi[...], a_lo[...]), NT) * rho
         total = product(split(covar), (w_hi[...], w_lo[...]), NN)
         out_ref[l] = total[EDGE : rows - EDGE]
-        stores.append(pltpu.make_async_copy(out_ref.at[l], out_hbm.at[l, pl.ds(EDGE, rows - 2 * EDGE)], out_sem.at[l]))
+        stores.append(pltpu.make_async_copy(out_ref.at[l], out_hbm.at[l, pl.ds(EDGE, middle)], out_sem.at[l]))
         stores[-1].start()
-        here = pl.ds(l * EDGE, EDGE)
         for side, part in enumerate((slice(0, EDGE), slice(rows - EDGE, rows))):
-            edge_ref[side, here, :] = total[part]
-            s_hi[side, here, :] = high[part]
-            s_lo[side, here, :] = low[part]
+            edge_ref[side, pl.ds(l * EDGE, EDGE), :] = total[part]
     for store in stores:
         store.wait()
 
@@ -209,7 +216,15 @@
             groups.append(cells)
         cells = jnp.concatenate(groups, axis=1)[:, : blocks * CAP]
         rho = taper(starts[s], EDGE, cells, shift) / (members - 1)
-        covar = product((s_hi[s], s_lo[s]), anom, NT)
+        high, low = (
+            jnp.concatenate([ref[l * columns + starts[s] : l * columns + starts[s] + EDGE, :] for l in range(levels)], axis=0)
+            for ref in (s_hi, s_lo)
+        )
+        both = jnp.concatenate(anom, axis=0)
+        dot = functools.partial(lax.dot_general, dimension_numbers=(NT, ((), ())), preferred_element_type=jnp.float32)
+        wide_dot = dot(high, both)
+        count = blocks * CAP
+        covar = wide_dot[:, :count] + (wide_dot[:, count:] + dot(low, anom[0]))
         covar = (covar.reshape(levels, EDGE, -1) * rho[None]).reshape(levels * EDGE, -1)
         out_ref[s] = edge_ref[s] + joined(split(covar), weight, NN)
         for l in range(levels):
@@ -264,22 +279,30 @@
     bf16 = jnp.bfloat16
     middle = columns - 2 * EDGE
     edges = (2, levels * EDGE, members)
-    total, *kept = pl.pallas_call(
+    halves = (levels * columns, members)
+    s_hi, s_lo = pl.pallas_call(
+        prep_kernel,
+        out_shape=[jax.ShapeDtypeStruct(halves, bf16)] * 2,
+        in_specs=[HBM],
+        out_specs=[VMEM] * 2,
+        scratch_shapes=[pltpu.VMEM(state.shape, f32), pltpu.SemaphoreType.DMA((levels,))],
+        compiler_params=limit(8),
+        name="prep",
+    )(*in_hbm(state))
+    total, edge = pl.pallas_call(
         functools.partial(own_kernel, blocks),
-        out_shape=[jax.ShapeDtypeStruct(state.shape, f32), jax.ShapeDtypeStruct(edges, f32)]
-        + [jax.ShapeDtypeStruct(edges, bf16)] * 2,
-        in_specs=[HBM] + [VMEM] * blocks,
-        out_specs=[HBM] + [VMEM] * 3,
-        scratch_shapes=[pltpu.VMEM(state.shape, f32), pltpu.VMEM((levels, middle, members), f32)]
+        out_shape=[jax.ShapeDtypeStruct(state.shape, f32), jax.ShapeDtypeStruct(edges, f32)],
+        in_specs=[VMEM] * (2 + blocks),
+        out_specs=[HBM, VMEM],
+        scratch_shapes=[pltpu.VMEM((levels, middle, members), f32)]
         + [pltpu.VMEM((obs, members), bf16)] * 4
-        + [pltpu.VMEM((columns, obs), f32)]
-        + [pltpu.SemaphoreType.DMA((levels,))] * 2,
+        + [pltpu.SemaphoreType.DMA((levels,))],
         cost_estimate=pl.CostEstimate(
             flops=12 * levels * columns * obs * members, bytes_accessed=8 * state.size + 8 * obs * members, transcendentals=0
         ),
         compiler_params=limit(24),
         name="own",
-    )(*in_hbm(state), *packs)
+    )(s_hi, s_lo, *packs)
     out = pl.pallas_call(
         functools.partial(halo_kernel, blocks),
         out_shape=jax.ShapeDtypeStruct(state.shape, f32),
@@ -289,7 +312,7 @@
         input_output_aliases={0: 0},
         compiler_params=limit(16),
         name="halo",
-    )(total, *kept, *halos)
+    )(total, edge, s_hi, s_lo, *halos)
     return out[None]
 
 

time: 39.9 us -> 38.1 us (0.955)
  waiting for transfers between devices: 7.75 us -> 6.8 us
  Pallas kernels: 9.43 us -> 8.58 us
    pallas_call x1, Pallas kernels: 5.99 us -> 3.76 us  [on_device(): pl.pallas_call(functools.partial(own_kernel, blocks), out_shape=[jax.Shap...]
    pallas_call x0 -> x1, Pallas kernels: none -> 1.64 us  [on_device(): pl.pallas_call(prep_kernel, out_shape=[jax.ShapeDtypeStruct(halves, bf16)...]
    ppermute x13, waiting for transfers between devices: 7.75 us -> 6.8 us  [exchange(): lax.ppermute(value, axis, [(i, target(i, step, size)) for i in range(size)])]
  transfers between devices with their start and end apart: 13 -> 13, of which waited for: 4 -> 5; matrix products, arithmetic and copies ran while one was open for 0% -> 0% of each run, Pallas kernels for 15% -> 14%
where the time goes in v2:
time: 38.1 us; the launch traced here: 37.9 us
  starting transfers between devices  22.5 us (59%)
  Pallas kernels  8.58 us (23%)
  waiting for transfers between devices  6.8 us (18%)
    ppermute x13, starting transfers between devices, exchange(): lax.ppermute(value, axis, [(i, target(i, step, size)) for i in range(size)])  22.5 us
    ppermute x13, waiting for transfers between devices, exchange(): lax.ppermute(value, axis, [(i, target(i, step, size)) for i in range(size)])  6.8 us
    pallas_call x1, Pallas kernels, on_device(): pl.pallas_call(functools.partial(own_kernel, blocks), out_shape=[jax.Shap...  3.76 us
    pallas_call x1, Pallas kernels, on_device(): pl.pallas_call(functools.partial(halo_kernel, blocks), out_shape=jax.Shap...  2.06 us
    pallas_call x1, Pallas kernels, on_device(): pl.pallas_call(prep_kernel, out_shape=[jax.ShapeDtypeStruct(halves, bf16)...  1.64 us
    pallas_call x1, Pallas kernels, on_device(): pl.pallas_call(pack_kernel, out_shape=[jax.ShapeDtypeStruct((SUB, 2 * (co...  1.07 us
  transfers between devices with their start and end apart: 13, of which 5 were waited for; matrix products, arithmetic and copies ran while one was open for 0% of the time, Pallas kernels for 14%

profile of v2, /device:TPU:0, one launch (start us, length us, event | category | flops | bytes accessed | tf_op | source)
XLA Modules:
  0.0 37.9 jit_solution(14364317107527011732)
XLA Ops:
  0.0 1.1 %pack.1 = (f32[8,8320]{1,0:T(8,128)S(1)}, s32[2,8,128]{2,1,0:T(8,128)S(1)}, f32[8,2176]{1,0:T(8,128)S(1)}, f32[8,2176]{1,0:T(8,128)S(1)}, f32[8,2176]{1,0:T(8,12...) custom-call(s32[8]{0:T(128)} %sector_hbm.1, ...), custom_call_target="tpu_custom_call" | custom-call | tf_op jit(solution)/shard_map/pack/pallas_call | solution.py:248
  1.1 0.6 %collective-permute-start.3 = (f32[8,2176]{1,0:T(8,128)S(1)}, f32[8,2176]{1,0:T(8,128)S(1)}, u32[]{:S(2)}, u32[]{:S(2)}) collective-permute-start(f32[8,2176]{1,0:T(8,128)S(1)} %get-tuple-element.24), channel_id=1, source_target_pairs={{0,4},{4,0},{8,12},{12,8},{16,20},{20,16},{24,28},{28,24},{1,5},{5... | collective-permute-start | bytes 208904 | tf_op jit(solution)/shard_map/ppermute | solution.py:41
  1.6 3.5 %collective-permute-start.2 = (f32[8,8320]{1,0:T(8,128)S(1)}, f32[8,8320]{1,0:T(8,128)S(1)}, u32[]{:S(2)}, u32[]{:S(2)}) collective-permute-start(f32[8,8320]{1,0:T(8,128)S(1)} %get-tuple-element.20.refs_0_), channel_id=1, source_target_pairs={{0,3},{1,2},{2,1},{3,0},{4,7},{5,6},{6,5},{7,4},{8,11},{9,10},{10,... | collective-permute-start | bytes 798728 | tf_op jit(solution)/shard_map/ppermute | solution.py:41
  5.1 0.5 %collective-permute-start.1 = (f32[8,8320]{1,0:T(8,128)S(1)}, f32[8,8320]{1,0:T(8,128)S(1)}, u32[]{:S(2)}, u32[]{:S(2)}) collective-permute-start(f32[8,8320]{1,0:T(8,128)S(1)} %get-tuple-element.20.refs_0_), channel_id=1, source_target_pairs={{0,2},{1,3},{2,0},{3,1},{4,6},{5,7},{6,4},{7,5},{8,10},{9,11},{10,... | collective-permute-start | bytes 798728 | tf_op jit(solution)/shard_map/ppermute | solution.py:41
  5.6 0.1 collective-permute-start
  5.8 2.0 %collective-permute-start.4 = (f32[8,2176]{1,0:T(8,128)S(1)}, f32[8,2176]{1,0:T(8,128)S(1)}, u32[]{:S(2)}, u32[]{:S(2)}) collective-permute-start(f32[8,2176]{1,0:T(8,128)S(1)} %get-tuple-element.25), channel_id=1, source_target_pairs={{0,8},{4,12},{8,0},{12,4},{16,24},{20,28},{24,16},{28,20},{1,9},{5... | collective-permute-start | bytes 208904 | tf_op jit(solution)/shard_map/ppermute | solution.py:41
  7.8 0.0 collective-permute-done.3.refs_0_
  7.8 0.0 collective-permute-start.5
  7.8 2.3 %collective-permute-done.4.refs_1_ = f32[8,2176]{1,0:T(8,128)S(1)} collective-permute-done((f32[8,2176]{1,0:T(8,128)S(1)}, f32[8,2176]{1,0:T(8,128)S(1)}, u32[]{:S(2)}, u32[]{:S(2)}) %collective-permute-start.4) | collective-permute-done | bytes 69664 | tf_op jit(solution)/shard_map/ppermute | solution.py:41
  10.1 3.0 %collective-permute-start.6 = (f32[8,2176]{1,0:T(8,128)S(1)}, f32[8,2176]{1,0:T(8,128)S(1)}, u32[]{:S(2)}, u32[]{:S(2)}) collective-permute-start(f32[8,2176]{1,0:T(8,128)S(1)} %get-tuple-element.27), channel_id=1, source_target_pairs={{0,16},{4,20},{8,24},{12,28},{16,0},{20,4},{24,8},{28,12},{1,17},{... | collective-permute-start | bytes 208904 | tf_op jit(solution)/shard_map/ppermute | solution.py:41
  13.1 0.9 %collective-permute-start.7 = (f32[8,2176]{1,0:T(8,128)S(1)}, f32[8,2176]{1,0:T(8,128)S(1)}, u32[]{:S(2)}, u32[]{:S(2)}) collective-permute-start(f32[8,2176]{1,0:T(8,128)S(1)} %get-tuple-element.28), channel_id=1, source_target_pairs={{0,20},{4,16},{8,28},{12,24},{16,4},{20,0},{24,12},{28,8},{1,21},{... | collective-permute-start | bytes 208904 | tf_op jit(solution)/shard_map/ppermute | solution.py:41
  14.0 1.5 %collective-permute-done.6.refs_3_ = f32[8,2176]{1,0:T(8,128)S(1)} collective-permute-done((f32[8,2176]{1,0:T(8,128)S(1)}, f32[8,2176]{1,0:T(8,128)S(1)}, u32[]{:S(2)}, u32[]{:S(2)}) %collective-permute-start.6) | collective-permute-done | bytes 69664 | tf_op jit(solution)/shard_map/ppermute | solution.py:41
  15.5 6.7 %collective-permute-start.8 = (f32[8,2176]{1,0:T(8,128)S(1)}, f32[8,2176]{1,0:T(8,128)S(1)}, u32[]{:S(2)}, u32[]{:S(2)}) collective-permute-start(f32[8,2176]{1,0:T(8,128)S(1)} %get-tuple-element.29), channel_id=1, source_target_pairs={{0,24},{4,28},{8,16},{12,20},{16,8},{20,12},{24,0},{28,4},{1,25},{... | collective-permute-start | bytes 208904 | tf_op jit(solution)/shard_map/ppermute | solution.py:41
  22.2 1.6 %collective-permute-start.9 = (f32[8,2176]{1,0:T(8,128)S(1)}, f32[8,2176]{1,0:T(8,128)S(1)}, u32[]{:S(2)}, u32[]{:S(2)}) collective-permute-start(f32[8,2176]{1,0:T(8,128)S(1)} %get-tuple-element.30), channel_id=1, source_target_pairs={{0,28},{4,24},{8,20},{12,16},{16,12},{20,8},{24,4},{28,0},{1,29},{... | collective-permute-start | bytes 208904 | tf_op jit(solution)/shard_map/ppermute | solution.py:41
  23.8 1.6 %prep.1 = (bf16[1024,512]{1,0:T(8,128)(2,1)S(1)}, bf16[1024,512]{1,0:T(8,128)(2,1)S(1)}) custom-call(f32[4,256,512]{2,1,0:T(8,128)} %bitcast.2), custom_call_target="tpu_custom_call" | custom-call | tf_op jit(solution)/shard_map/prep/pallas_call | solution.py:283
  25.5 2.3 %collective-permute-done.9.refs_6_ = f32[8,2176]{1,0:T(8,128)S(1)} collective-permute-done((f32[8,2176]{1,0:T(8,128)S(1)}, f32[8,2176]{1,0:T(8,128)S(1)}, u32[]{:S(2)}, u32[]{:S(2)}) %collective-permute-start.9) | collective-permute-done | bytes 69664 | tf_op jit(solution)/shard_map/ppermute | solution.py:41
  27.8 0.1 pick.1.refs_0_
  27.8 2.5 %collective-permute-start.12 = (f32[8,4352]{1,0:T(8,128)S(1)}, f32[8,4352]{1,0:T(8,128)S(1)}, u32[]{:S(2)}, u32[]{:S(2)}) collective-permute-start(f32[8,4352]{1,0:T(8,128)S(1)} %pick.1.refs_0_), channel_id=1, source_target_pairs={{0,3},{1,2},{2,1},{3,0},{4,7},{5,6},{6,5},{7,4},{8,11},{9,10},{10,... | collective-permute-start | bytes 417800 | tf_op jit(solution)/shard_map/ppermute | solution.py:41
  30.3 0.5 %collective-permute-start.11 = (f32[8,4352]{1,0:T(8,128)S(1)}, f32[8,4352]{1,0:T(8,128)S(1)}, u32[]{:S(2)}, u32[]{:S(2)}) collective-permute-start(f32[8,4352]{1,0:T(8,128)S(1)} %pick.1.refs_0_), channel_id=1, source_target_pairs={{0,2},{1,3},{2,0},{3,1},{4,6},{5,7},{6,4},{7,5},{8,10},{9,11},{10,... | collective-permute-start | bytes 417800 | tf_op jit(solution)/shard_map/ppermute | solution.py:41
  30.8 0.6 %collective-permute-start.10 = (f32[8,4352]{1,0:T(8,128)S(1)}, f32[8,4352]{1,0:T(8,128)S(1)}, u32[]{:S(2)}, u32[]{:S(2)}) collective-permute-start(f32[8,4352]{1,0:T(8,128)S(1)} %pick.1.refs_0_), channel_id=1, source_target_pairs={{0,1},{1,0},{2,3},{3,2},{4,5},{5,4},{6,7},{7,6},{8,9},{9,8},{10,11... | collective-permute-start | bytes 417800 | tf_op jit(solution)/shard_map/ppermute | solution.py:41
  31.4 3.8 %own.1 = (f32[4,256,512]{2,1,0:T(8,128)}, f32[2,256,512]{2,1,0:T(8,128)S(1)}) custom-call(bf16[1024,512]{1,0:T(8,128)(2,1)S(1)} %get-tuple-element.18.s_hi, bf16[1024,512]{1,0:T(8,128)(2,1)S(1)} %get-tuple-element.19.s_lo, f32[8,8320]{1,0:T(8,128)S(1)} %get-tuple-element.20.refs_0_, f32[8,8320]{1,0:T(8,128)S(1)} %collective-permute-done.refs_1_, ...), custom_call_target="tpu_custom_call" | custom-call | flops 1610612736 | bytes 5242880 | tf_op jit(solution)/shard_map/own/pallas_call | solution.py:292
  35.2 0.5 %collective-permute-done.11.refs_2_ = f32[8,4352]{1,0:T(8,128)S(1)} collective-permute-done((f32[8,4352]{1,0:T(8,128)S(1)}, f32[8,4352]{1,0:T(8,128)S(1)}, u32[]{:S(2)}, u32[]{:S(2)}) %collective-permute-start.11) | collective-permute-done | bytes 139296 | tf_op jit(solution)/shard_map/ppermute | solution.py:41
  35.7 0.2 collective-permute-done.10.refs_1_
  35.9 2.1 %halo.1 = f32[4,256,512]{2,1,0:T(8,128)} custom-call(f32[4,256,512]{2,1,0:T(8,128)} %get-tuple-element.21.total_hbm, f32[2,256,512]{2,1,0:T(8,128)S(1)} %get-tuple-element.22.edge_ref, bf16[1024,512]{1,0:T(8,128)(2,1)S(1)} %get-tuple-element.18.s_hi, bf16[1024,512]{1,0:T(8,128)(2,1)S(1)} %get-tuple-element.19.s_lo, ...), custom_call_target="tpu_custom_call", output_to_operand_aliasing={{}: (0, {})} | custom-call | tf_op jit(solution)/shard_map/halo/pallas_call | solution.py:306
  (7 shorter events, 0.0 us)
Async XLA Ops:
  1.1 6.7 %collective-permute-start.3 = (f32[8,2176]{1,0:T(8,128)S(1)}, f32[8,2176]{1,0:T(8,128)S(1)}, u32[]{:S(2)}, u32[]{:S(2)}) collective-permute-start(f32[8,2176]{1,0:T(8,128)S(1)} %get-tuple-element.24), channel_id=1, source_target_pairs={{0,4},{4,0},{8,12},{12,8},{16,20},{20,16},{24,28},{28,24},{1,5},{5... | collective-permute-start | bytes 208904 | tf_op jit(solution)/shard_map/ppermute | solution.py:41
  1.6 29.2 %collective-permute-start.2 = (f32[8,8320]{1,0:T(8,128)S(1)}, f32[8,8320]{1,0:T(8,128)S(1)}, u32[]{:S(2)}, u32[]{:S(2)}) collective-permute-start(f32[8,8320]{1,0:T(8,128)S(1)} %get-tuple-element.20.refs_0_), channel_id=1, source_target_pairs={{0,3},{1,2},{2,1},{3,0},{4,7},{5,6},{6,5},{7,4},{8,11},{9,10},{10,... | collective-permute-start | bytes 798728 | tf_op jit(solution)/shard_map/ppermute | solution.py:41
  5.1 26.3 %collective-permute-start.1 = (f32[8,8320]{1,0:T(8,128)S(1)}, f32[8,8320]{1,0:T(8,128)S(1)}, u32[]{:S(2)}, u32[]{:S(2)}) collective-permute-start(f32[8,8320]{1,0:T(8,128)S(1)} %get-tuple-element.20.refs_0_), channel_id=1, source_target_pairs={{0,2},{1,3},{2,0},{3,1},{4,6},{5,7},{6,4},{7,5},{8,10},{9,11},{10,... | collective-permute-start | bytes 798728 | tf_op jit(solution)/shard_map/ppermute | solution.py:41
  5.6 25.8 %collective-permute-start = (f32[8,8320]{1,0:T(8,128)S(1)}, f32[8,8320]{1,0:T(8,128)S(1)}, u32[]{:S(2)}, u32[]{:S(2)}) collective-permute-start(f32[8,8320]{1,0:T(8,128)S(1)} %get-tuple-element.20.refs_0_), channel_id=1, source_target_pairs={{0,1},{1,0},{2,3},{3,2},{4,5},{5,4},{6,7},{7,6},{8,9},{9,8},{10,11... | collective-permute-start | bytes 798728 | tf_op jit(solution)/shard_map/ppermute | solution.py:41
  5.8 4.3 %collective-permute-start.4 = (f32[8,2176]{1,0:T(8,128)S(1)}, f32[8,2176]{1,0:T(8,128)S(1)}, u32[]{:S(2)}, u32[]{:S(2)}) collective-permute-start(f32[8,2176]{1,0:T(8,128)S(1)} %get-tuple-element.25), channel_id=1, source_target_pairs={{0,8},{4,12},{8,0},{12,4},{16,24},{20,28},{24,16},{28,20},{1,9},{5... | collective-permute-start | bytes 208904 | tf_op jit(solution)/shard_map/ppermute | solution.py:41
  7.8 5.3 %collective-permute-start.5 = (f32[8,2176]{1,0:T(8,128)S(1)}, f32[8,2176]{1,0:T(8,128)S(1)}, u32[]{:S(2)}, u32[]{:S(2)}) collective-permute-start(f32[8,2176]{1,0:T(8,128)S(1)} %get-tuple-element.26), channel_id=1, source_target_pairs={{0,12},{4,8},{8,4},{12,0},{16,28},{20,24},{24,20},{28,16},{1,13},{... | collective-permute-start | bytes 208904 | tf_op jit(solution)/shard_map/ppermute | solution.py:41
  10.1 5.4 %collective-permute-start.6 = (f32[8,2176]{1,0:T(8,128)S(1)}, f32[8,2176]{1,0:T(8,128)S(1)}, u32[]{:S(2)}, u32[]{:S(2)}) collective-permute-start(f32[8,2176]{1,0:T(8,128)S(1)} %get-tuple-element.27), channel_id=1, source_target_pairs={{0,16},{4,20},{8,24},{12,28},{16,0},{20,4},{24,8},{28,12},{1,17},{... | collective-permute-start | bytes 208904 | tf_op jit(solution)/shard_map/ppermute | solution.py:41
  13.1 9.2 %collective-permute-start.7 = (f32[8,2176]{1,0:T(8,128)S(1)}, f32[8,2176]{1,0:T(8,128)S(1)}, u32[]{:S(2)}, u32[]{:S(2)}) collective-permute-start(f32[8,2176]{1,0:T(8,128)S(1)} %get-tuple-element.28), channel_id=1, source_target_pairs={{0,20},{4,16},{8,28},{12,24},{16,4},{20,0},{24,12},{28,8},{1,21},{... | collective-permute-start | bytes 208904 | tf_op jit(solution)/shard_map/ppermute | solution.py:41
  15.5 10.0 %collective-permute-start.8 = (f32[8,2176]{1,0:T(8,128)S(1)}, f32[8,2176]{1,0:T(8,128)S(1)}, u32[]{:S(2)}, u32[]{:S(2)}) collective-permute-start(f32[8,2176]{1,0:T(8,128)S(1)} %get-tuple-element.29), channel_id=1, source_target_pairs={{0,24},{4,28},{8,16},{12,20},{16,8},{20,12},{24,0},{28,4},{1,25},{... | collective-permute-start | bytes 208904 | tf_op jit(solution)/shard_map/ppermute | solution.py:41
  22.2 5.5 %collective-permute-start.9 = (f32[8,2176]{1,0:T(8,128)S(1)}, f32[8,2176]{1,0:T(8,128)S(1)}, u32[]{:S(2)}, u32[]{:S(2)}) collective-permute-start(f32[8,2176]{1,0:T(8,128)S(1)} %get-tuple-element.30), channel_id=1, source_target_pairs={{0,28},{4,24},{8,20},{12,16},{16,12},{20,8},{24,4},{28,0},{1,29},{... | collective-permute-start | bytes 208904 | tf_op jit(solution)/shard_map/ppermute | solution.py:41
  27.8 7.3 %collective-permute-start.12 = (f32[8,4352]{1,0:T(8,128)S(1)}, f32[8,4352]{1,0:T(8,128)S(1)}, u32[]{:S(2)}, u32[]{:S(2)}) collective-permute-start(f32[8,4352]{1,0:T(8,128)S(1)} %pick.1.refs_0_), channel_id=1, source_target_pairs={{0,3},{1,2},{2,1},{3,0},{4,7},{5,6},{6,5},{7,4},{8,11},{9,10},{10,... | collective-permute-start | bytes 417800 | tf_op jit(solution)/shard_map/ppermute | solution.py:41
  30.3 5.4 %collective-permute-start.11 = (f32[8,4352]{1,0:T(8,128)S(1)}, f32[8,4352]{1,0:T(8,128)S(1)}, u32[]{:S(2)}, u32[]{:S(2)}) collective-permute-start(f32[8,4352]{1,0:T(8,128)S(1)} %pick.1.refs_0_), channel_id=1, source_target_pairs={{0,2},{1,3},{2,0},{3,1},{4,6},{5,7},{6,4},{7,5},{8,10},{9,11},{10,... | collective-permute-start | bytes 417800 | tf_op jit(solution)/shard_map/ppermute | solution.py:41
  30.8 5.1 %collective-permute-start.10 = (f32[8,4352]{1,0:T(8,128)S(1)}, f32[8,4352]{1,0:T(8,128)S(1)}, u32[]{:S(2)}, u32[]{:S(2)}) collective-permute-start(f32[8,4352]{1,0:T(8,128)S(1)} %pick.1.refs_0_), channel_id=1, source_target_pairs={{0,1},{1,0},{2,3},{3,2},{4,5},{5,4},{6,7},{7,6},{8,9},{9,8},{10,11... | collective-permute-start | bytes 417800 | tf_op jit(solution)/shard_map/ppermute | solution.py:41

commit v3 on v2

--- a/solution.py
+++ b/solution.py
@@ -28,10 +28,6 @@
     return [pltpu.with_memory_space_constraint(value, pltpu.HBM) for value in values]
 
 
-def partner(index, step, size):
-    return index ^ step if size & (size - 1) == 0 else (index + size - step) % size
-
-
 def target(index, step, size):
     return index ^ step if size & (size - 1) == 0 else (index + step) % size
 
@@ -84,7 +80,7 @@
 
 
 def pack_kernel(sector_hbm, anom_hbm, weight_hbm, cell_hbm, own_ref, *refs):
-    side_ref, *slot_refs, sector_ref, anom_ref, weight_ref, cell_ref, sems = refs
+    side_ref, cross_ref, *near_refs, sector_ref, anom_ref, weight_ref, cell_ref, sems = refs
     count, members = weight_ref.shape
     loads = [
         pltpu.make_async_copy(cell_hbm, cell_ref, sems.at[0]),
@@ -95,6 +91,7 @@
     for load in loads:
         load.start()
     regions = lax.axis_size("region")
+    half_way = regions // 2
     me = lax.axis_index("region")
     entry = lax.broadcasted_iota(jnp.int32, (count, LANES), 0)
     lane = lax.broadcasted_iota(jnp.int32, (count, LANES), 1)
@@ -107,14 +104,20 @@
     spread = [lax.dot_general(cells, pick, (NN, ((), ())), preferred_element_type=jnp.float32) for pick in picks]
     loads[1].wait()
     mine = sector_ref[me]
-    to_right, from_left, from_right = [], jnp.int32(0), jnp.int32(0)
+    far = me ^ half_way
+    is_next = lambda first, second: second == lax.rem(first + 1, regions)
+    from_left, from_right, to_right = jnp.int32(0), jnp.int32(0), []
     for step in range(1, regions):
-        to_right.append(sector_ref[target(me, step, regions)] == lax.rem(mine + 1, regions))
-        sector = sector_ref[partner(me, step, regions)]
-        from_left = jnp.where(sector == lax.rem(mine + regions - 1, regions), step, from_left)
-        from_right = jnp.where(sector == lax.rem(mine + 1, regions), step, from_right)
-    side_ref[0] = jnp.broadcast_to(from_left, (SUB, LANES))
-    side_ref[1] = jnp.broadcast_to(from_right, (SUB, LANES))
+        sector = sector_ref[me ^ step]
+        from_left = jnp.where(is_next(sector, mine), step, from_left)
+        from_right = jnp.where(is_next(mine, sector), step, from_right)
+    codes = [from_left, from_right]
+    for step in range(1, half_way):
+        sector = sector_ref[me ^ step]
+        to_right.append(is_next(mine, sector))
+        codes.append(is_next(sector_ref[far], sector).astype(jnp.int32))
+    for i, code in enumerate(codes):
+        side_ref[i] = jnp.broadcast_to(code, (SUB, LANES))
     for load in loads[2:]:
         load.wait()
     half = count // SUB * members
@@ -124,20 +127,35 @@
     low = (folded(anom_ref[:CAP, :]), folded(weight_ref[:CAP, :]), spread[1])
     high = (folded(anom_ref[count - CAP :, :]), folded(weight_ref[count - CAP :, :]), spread[2])
     wide = CAP // SUB * members
-    for slot, up in zip(slot_refs, to_right):
-        for (start, stop), lo, hi in zip(((0, wide), (wide, 2 * wide), (2 * wide, 2 * wide + LANES)), low, high):
-            slot[:, start:stop] = jnp.where(up, hi, lo)
-
-
-def pick_kernel(side_ref, *refs):
+    width = 2 * wide + LANES
+    for (start, stop), lo, hi in zip(((0, wide), (wide, 2 * wide), (2 * wide, width)), low, high):
+        cross_ref[:, start:stop] = lo
+        cross_ref[:, width + start : width + stop] = hi
+        for near, up in zip(near_refs, to_right):
+            near[:, start:stop] = jnp.where(up, hi, lo)
+
+
+def relay_kernel(side_ref, cross_ref, *pass_refs):
+    width = pass_refs[0].shape[1]
+    for step, out in enumerate(pass_refs, start=1):
+        up = side_ref[1 + step] == 1
+        for at in range(0, width, LANES):
+            out[:, at : at + LANES] = jnp.where(up, cross_ref[:, width + at : width + at + LANES], cross_ref[:, at : at + LANES])
+
+
+def pick_kernel(side_ref, cross_ref, *refs):
     *slot_refs, halo_ref = refs
     width = slot_refs[0].shape[1]
+    half_way = len(slot_refs) // 2 + 1
+    near, passed = slot_refs[: half_way - 1], slot_refs[half_way - 1 :]
     for side in range(2):
-        step_of = side_ref[side]
+        code = side_ref[side]
         for at in range(0, width, LANES):
-            value = slot_refs[0][:, at : at + LANES]
-            for step, slot in enumerate(slot_refs[1:], start=2):
-                value = jnp.where(step_of == step, slot[:, at : at + LANES], value)
+            here = (1 - side) * width + at
+            value = cross_ref[:, here : here + LANES]
+            for step in range(1, half_way):
+                value = jnp.where(code == step, near[step - 1][:, at : at + LANES], value)
+                value = jnp.where(code == step + half_way, passed[step - 1][:, at : at + LANES], value)
             halo_ref[:, side * width + at : side * width + at + LANES] = value
 
 
@@ -244,14 +262,18 @@
     count = obs_anom.shape[1]
     blocks = owners
 
+    assert regions & (regions - 1) == 0
+    half_way = regions // 2
     slot = jax.ShapeDtypeStruct((SUB, 2 * (CAP // SUB) * members + LANES), f32)
-    own_pack, sides, *slots = pl.pallas_call(
+    pair = jax.ShapeDtypeStruct((SUB, 2 * slot.shape[1]), f32)
+    near = range(1, half_way)
+    own_pack, sides, cross, *slots = pl.pallas_call(
         pack_kernel,
         out_shape=[jax.ShapeDtypeStruct((SUB, 2 * (count // SUB) * members + LANES), f32)]
-        + [jax.ShapeDtypeStruct((2, SUB, LANES), jnp.int32)]
-        + [slot] * (regions - 1),
+        + [jax.ShapeDtypeStruct((half_way + 1, SUB, LANES), jnp.int32), pair]
+        + [slot] * len(near),
         in_specs=[HBM] * 4,
-        out_specs=[VMEM] * (regions + 1),
+        out_specs=[VMEM] * (3 + len(near)),
         scratch_shapes=[
             pltpu.SMEM((regions,), jnp.int32),
             pltpu.VMEM((count, members), f32),
@@ -262,16 +284,26 @@
         compiler_params=limit(8),
         name="pack",
     )(*in_hbm(sector_of, obs_anom, obs_weight, obs_cell))
-    got = [exchange(slots[k - 1], "region", k) for k in range(1, regions)]
+    crossed = exchange(cross, "region", half_way)
+    direct = [exchange(slots[k - 1], "region", k) for k in near]
+    relayed = pl.pallas_call(
+        relay_kernel,
+        out_shape=[slot] * len(near),
+        in_specs=[VMEM] * 2,
+        out_specs=[VMEM] * len(near),
+        compiler_params=limit(4),
+        name="relay",
+    )(sides, crossed)
+    passed = [exchange(relayed[k - 1], "region", k) for k in near]
     packs = [own_pack] + [exchange(own_pack, "state", k) for k in range(1, owners)]
     halo = pl.pallas_call(
         pick_kernel,
-        out_shape=jax.ShapeDtypeStruct((SUB, 2 * slot.shape[1]), f32),
-        in_specs=[VMEM] * regions,
+        out_shape=pair,
+        in_specs=[VMEM] * (2 + 2 * len(near)),
         out_specs=VMEM,
         compiler_params=limit(4),
         name="pick",
-    )(sides, *got)
+    )(sides, crossed, *direct, *passed)
     halos = [halo] + [exchange(halo, "state", k) for k in range(1, owners)]
 
     obs = blocks * count

time: 38.1 us -> 35.1 us (0.921)
  starting transfers between devices: 22.5 us -> 13.9 us
  waiting for transfers between devices: 6.8 us -> 12.4 us
    ppermute x13, starting transfers between devices: 22.5 us -> 13.9 us  [exchange(): lax.ppermute(value, axis, [(i, target(i, step, size)) for i in range(size)])]
    ppermute x13, waiting for transfers between devices: 6.8 us -> 12.4 us  [exchange(): lax.ppermute(value, axis, [(i, target(i, step, size)) for i in range(size)])]
  transfers between devices with their start and end apart: 13 -> 13, of which waited for: 5 -> 7; matrix products, arithmetic and copies ran while one was open for 0% -> 0% of each run, Pallas kernels for 14% -> 16%
where the time goes in v3:
time: 35.1 us; the launch traced here: 35 us
  starting transfers between devices  13.9 us (40%)
  waiting for transfers between devices  12.4 us (35%)
  Pallas kernels  8.59 us (24%)
    ppermute x13, starting transfers between devices, exchange(): lax.ppermute(value, axis, [(i, target(i, step, size)) for i in range(size)])  13.9 us
    ppermute x13, waiting for transfers between devices, exchange(): lax.ppermute(value, axis, [(i, target(i, step, size)) for i in range(size)])  12.4 us
    pallas_call x1, Pallas kernels, on_device(): pl.pallas_call(functools.partial(own_kernel, blocks), out_shape=[jax.Shap...  3.76 us
    pallas_call x1, Pallas kernels, on_device(): pl.pallas_call(functools.partial(halo_kernel, blocks), out_shape=jax.Shap...  2.05 us
    pallas_call x1, Pallas kernels, on_device(): pl.pallas_call(prep_kernel, out_shape=[jax.ShapeDtypeStruct(halves, bf16)...  1.64 us
    pallas_call x1, Pallas kernels, on_device(): pl.pallas_call(pack_kernel, out_shape=[jax.ShapeDtypeStruct((SUB, 2 * (co...  1.06 us
  transfers between devices with their start and end apart: 13, of which 7 were waited for; matrix products, arithmetic and copies ran while one was open for 0% of the time, Pallas kernels for 16%

profile of v3, /device:TPU:0, one launch (start us, length us, event | category | flops | bytes accessed | tf_op | source)
XLA Modules:
  0.0 35.0 jit_solution(13542657630120198269)
XLA Ops:
  0.0 1.1 %pack.1 = (f32[8,8320]{1,0:T(8,128)S(1)}, s32[5,8,128]{2,1,0:T(8,128)S(1)}, f32[8,4352]{1,0:T(8,128)S(1)}, f32[8,2176]{1,0:T(8,128)S(1)}, f32[8,2176]{1,0:T(8,128)S(1)}, /*index=5*/f32[8,2176]{1,0:T(8,128)S(1)}) custom-call(s32[8]{0:T(128)} %sector_hbm.1, f32[1,64,512]{2,1,0:T(8,128)} %anom_hbm.1, f32[1,64,512]{2,1,0:T(8,128)} %weight_hbm.1, s32[1,64]{1,0:T(1,128)} %cell_hbm.1), custom_call_target="tpu_custom_call" | custom-call | tf_op jit(solution)/shard_map/pack/pallas_call | solution.py:270
  1.1 4.1 %collective-permute-start.3 = (f32[8,4352]{1,0:T(8,128)S(1)}, f32[8,4352]{1,0:T(8,128)S(1)}, u32[]{:S(2)}, u32[]{:S(2)}) collective-permute-start(f32[8,4352]{1,0:T(8,128)S(1)} %get-tuple-element.24), channel_id=1, source_target_pairs={{0,16},{4,20},{8,24},{12,28},{16,0},{20,4},{24,8},{28,12},{1,17},{... | collective-permute-start | bytes 417800 | tf_op jit(solution)/shard_map/ppermute | solution.py:37
  5.2 2.4 %collective-permute-start.2 = (f32[8,8320]{1,0:T(8,128)S(1)}, f32[8,8320]{1,0:T(8,128)S(1)}, u32[]{:S(2)}, u32[]{:S(2)}) collective-permute-start(f32[8,8320]{1,0:T(8,128)S(1)} %get-tuple-element.20.refs_0_), channel_id=1, source_target_pairs={{0,3},{1,2},{2,1},{3,0},{4,7},{5,6},{6,5},{7,4},{8,11},{9,10},{10,... | collective-permute-start | bytes 798728 | tf_op jit(solution)/shard_map/ppermute | solution.py:37
  7.6 0.5 %collective-permute-start.1 = (f32[8,8320]{1,0:T(8,128)S(1)}, f32[8,8320]{1,0:T(8,128)S(1)}, u32[]{:S(2)}, u32[]{:S(2)}) collective-permute-start(f32[8,8320]{1,0:T(8,128)S(1)} %get-tuple-element.20.refs_0_), channel_id=1, source_target_pairs={{0,2},{1,3},{2,0},{3,1},{4,6},{5,7},{6,4},{7,5},{8,10},{9,11},{10,... | collective-permute-start | bytes 798728 | tf_op jit(solution)/shard_map/ppermute | solution.py:37
  8.2 0.5 %collective-permute-start = (f32[8,8320]{1,0:T(8,128)S(1)}, f32[8,8320]{1,0:T(8,128)S(1)}, u32[]{:S(2)}, u32[]{:S(2)}) collective-permute-start(f32[8,8320]{1,0:T(8,128)S(1)} %get-tuple-element.20.refs_0_), channel_id=1, source_target_pairs={{0,1},{1,0},{2,3},{3,2},{4,5},{5,4},{6,7},{7,6},{8,9},{9,8},{10,11... | collective-permute-start | bytes 798728 | tf_op jit(solution)/shard_map/ppermute | solution.py:37
  8.7 0.0 collective-permute-start.4
  8.7 3.2 %collective-permute-done.3.cross_ref = f32[8,4352]{1,0:T(8,128)S(1)} collective-permute-done((f32[8,4352]{1,0:T(8,128)S(1)}, f32[8,4352]{1,0:T(8,128)S(1)}, u32[]{:S(2)}, u32[]{:S(2)}) %collective-permute-start.3) | collective-permute-done | bytes 139296 | tf_op jit(solution)/shard_map/ppermute | solution.py:37
  11.9 0.7 %collective-permute-start.5 = (f32[8,2176]{1,0:T(8,128)S(1)}, f32[8,2176]{1,0:T(8,128)S(1)}, u32[]{:S(2)}, u32[]{:S(2)}) collective-permute-start(f32[8,2176]{1,0:T(8,128)S(1)} %get-tuple-element.26), channel_id=1, source_target_pairs={{0,8},{4,12},{8,0},{12,4},{16,24},{20,28},{24,16},{28,20},{1,9},{5... | collective-permute-start | bytes 208904 | tf_op jit(solution)/shard_map/ppermute | solution.py:37
  12.6 0.1 collective-permute-start.6
  12.7 4.0 %collective-permute-done.5.refs_1_ = f32[8,2176]{1,0:T(8,128)S(1)} collective-permute-done((f32[8,2176]{1,0:T(8,128)S(1)}, f32[8,2176]{1,0:T(8,128)S(1)}, u32[]{:S(2)}, u32[]{:S(2)}) %collective-permute-start.5) | collective-permute-done | bytes 69664 | tf_op jit(solution)/shard_map/ppermute | solution.py:37
  16.7 0.5 %collective-permute-done.6.refs_2_ = f32[8,2176]{1,0:T(8,128)S(1)} collective-permute-done((f32[8,2176]{1,0:T(8,128)S(1)}, f32[8,2176]{1,0:T(8,128)S(1)}, u32[]{:S(2)}, u32[]{:S(2)}) %collective-permute-start.6) | collective-permute-done | bytes 69664 | tf_op jit(solution)/shard_map/ppermute | solution.py:37
  17.2 1.2 %collective-permute-start.8 = (f32[8,2176]{1,0:T(8,128)S(1)}, f32[8,2176]{1,0:T(8,128)S(1)}, u32[]{:S(2)}, u32[]{:S(2)}) collective-permute-start(f32[8,2176]{1,0:T(8,128)S(1)} %get-tuple-element.29), channel_id=1, source_target_pairs={{0,8},{4,12},{8,0},{12,4},{16,24},{20,28},{24,16},{28,20},{1,9},{5... | collective-permute-start | bytes 208904 | tf_op jit(solution)/shard_map/ppermute | solution.py:37
  18.4 0.7 %collective-permute-start.9 = (f32[8,2176]{1,0:T(8,128)S(1)}, f32[8,2176]{1,0:T(8,128)S(1)}, u32[]{:S(2)}, u32[]{:S(2)}) collective-permute-start(f32[8,2176]{1,0:T(8,128)S(1)} %get-tuple-element.30), channel_id=1, source_target_pairs={{0,12},{4,8},{8,4},{12,0},{16,28},{20,24},{24,20},{28,16},{1,13},{... | collective-permute-start | bytes 208904 | tf_op jit(solution)/shard_map/ppermute | solution.py:37
  19.1 1.6 %prep.1 = (bf16[1024,512]{1,0:T(8,128)(2,1)S(1)}, bf16[1024,512]{1,0:T(8,128)(2,1)S(1)}) custom-call(f32[4,256,512]{2,1,0:T(8,128)} %bitcast.2), custom_call_target="tpu_custom_call" | custom-call | tf_op jit(solution)/shard_map/prep/pallas_call | solution.py:315
  20.8 1.4 %collective-permute-done.8.refs_4_ = f32[8,2176]{1,0:T(8,128)S(1)} collective-permute-done((f32[8,2176]{1,0:T(8,128)S(1)}, f32[8,2176]{1,0:T(8,128)S(1)}, u32[]{:S(2)}, u32[]{:S(2)}) %collective-permute-start.8) | collective-permute-done | bytes 69664 | tf_op jit(solution)/shard_map/ppermute | solution.py:37
  22.2 0.8 %collective-permute-done.9.refs_5_ = f32[8,2176]{1,0:T(8,128)S(1)} collective-permute-done((f32[8,2176]{1,0:T(8,128)S(1)}, f32[8,2176]{1,0:T(8,128)S(1)}, u32[]{:S(2)}, u32[]{:S(2)}) %collective-permute-start.9) | collective-permute-done | bytes 69664 | tf_op jit(solution)/shard_map/ppermute | solution.py:37
  23.0 0.1 pick.1.refs_0_
  23.1 2.6 %collective-permute-start.12 = (f32[8,4352]{1,0:T(8,128)S(1)}, f32[8,4352]{1,0:T(8,128)S(1)}, u32[]{:S(2)}, u32[]{:S(2)}) collective-permute-start(f32[8,4352]{1,0:T(8,128)S(1)} %pick.1.refs_0_), channel_id=1, source_target_pairs={{0,3},{1,2},{2,1},{3,0},{4,7},{5,6},{6,5},{7,4},{8,11},{9,10},{10,... | collective-permute-start | bytes 417800 | tf_op jit(solution)/shard_map/ppermute | solution.py:37
  25.7 0.5 %collective-permute-start.11 = (f32[8,4352]{1,0:T(8,128)S(1)}, f32[8,4352]{1,0:T(8,128)S(1)}, u32[]{:S(2)}, u32[]{:S(2)}) collective-permute-start(f32[8,4352]{1,0:T(8,128)S(1)} %pick.1.refs_0_), channel_id=1, source_target_pairs={{0,2},{1,3},{2,0},{3,1},{4,6},{5,7},{6,4},{7,5},{8,10},{9,11},{10,... | collective-permute-start | bytes 417800 | tf_op jit(solution)/shard_map/ppermute | solution.py:37
  26.2 0.4 %collective-permute-start.10 = (f32[8,4352]{1,0:T(8,128)S(1)}, f32[8,4352]{1,0:T(8,128)S(1)}, u32[]{:S(2)}, u32[]{:S(2)}) collective-permute-start(f32[8,4352]{1,0:T(8,128)S(1)} %pick.1.refs_0_), channel_id=1, source_target_pairs={{0,1},{1,0},{2,3},{3,2},{4,5},{5,4},{6,7},{7,6},{8,9},{9,8},{10,11... | collective-permute-start | bytes 417800 | tf_op jit(solution)/shard_map/ppermute | solution.py:37
  26.6 3.8 %own.1 = (f32[4,256,512]{2,1,0:T(8,128)}, f32[2,256,512]{2,1,0:T(8,128)S(1)}) custom-call(bf16[1024,512]{1,0:T(8,128)(2,1)S(1)} %get-tuple-element.18.s_hi, bf16[1024,512]{1,0:T(8,128)(2,1)S(1)} %get-tuple-element.19.s_lo, f32[8,8320]{1,0:T(8,128)S(1)} %get-tuple-element.20.refs_0_, f32[8,8320]{1,0:T(8,128)S(1)} %collective-permute-done.refs_1_, ...), custom_call_target="tpu_custom_call" | custom-call | flops 1610612736 | bytes 5242880 | tf_op jit(solution)/shard_map/own/pallas_call | solution.py:324
  30.4 2.4 %collective-permute-done.11.refs_2_ = f32[8,4352]{1,0:T(8,128)S(1)} collective-permute-done((f32[8,4352]{1,0:T(8,128)S(1)}, f32[8,4352]{1,0:T(8,128)S(1)}, u32[]{:S(2)}, u32[]{:S(2)}) %collective-permute-start.11) | collective-permute-done | bytes 139296 | tf_op jit(solution)/shard_map/ppermute | solution.py:37
  32.8 0.1 collective-permute-done.10.refs_1_
  32.9 2.1 %halo.1 = f32[4,256,512]{2,1,0:T(8,128)} custom-call(f32[4,256,512]{2,1,0:T(8,128)} %get-tuple-element.21.total_hbm, f32[2,256,512]{2,1,0:T(8,128)S(1)} %get-tuple-element.22.edge_ref, bf16[1024,512]{1,0:T(8,128)(2,1)S(1)} %get-tuple-element.18.s_hi, bf16[1024,512]{1,0:T(8,128)(2,1)S(1)} %get-tuple-element.19.s_lo, ...), custom_call_target="tpu_custom_call", output_to_operand_aliasing={{}: (0, {})} | custom-call | tf_op jit(solution)/shard_map/halo/pallas_call | solution.py:338
  (8 shorter events, 0.0 us)
Async XLA Ops:
  1.1 10.8 %collective-permute-start.3 = (f32[8,4352]{1,0:T(8,128)S(1)}, f32[8,4352]{1,0:T(8,128)S(1)}, u32[]{:S(2)}, u32[]{:S(2)}) collective-permute-start(f32[8,4352]{1,0:T(8,128)S(1)} %get-tuple-element.24), channel_id=1, source_target_pairs={{0,16},{4,20},{8,24},{12,28},{16,0},{20,4},{24,8},{28,12},{1,17},{... | collective-permute-start | bytes 417800 | tf_op jit(solution)/shard_map/ppermute | solution.py:37
  5.2 21.0 %collective-permute-start.2 = (f32[8,8320]{1,0:T(8,128)S(1)}, f32[8,8320]{1,0:T(8,128)S(1)}, u32[]{:S(2)}, u32[]{:S(2)}) collective-permute-start(f32[8,8320]{1,0:T(8,128)S(1)} %get-tuple-element.20.refs_0_), channel_id=1, source_target_pairs={{0,3},{1,2},{2,1},{3,0},{4,7},{5,6},{6,5},{7,4},{8,11},{9,10},{10,... | collective-permute-start | bytes 798728 | tf_op jit(solution)/shard_map/ppermute | solution.py:37
  7.6 19.0 %collective-permute-start.1 = (f32[8,8320]{1,0:T(8,128)S(1)}, f32[8,8320]{1,0:T(8,128)S(1)}, u32[]{:S(2)}, u32[]{:S(2)}) collective-permute-start(f32[8,8320]{1,0:T(8,128)S(1)} %get-tuple-element.20.refs_0_), channel_id=1, source_target_pairs={{0,2},{1,3},{2,0},{3,1},{4,6},{5,7},{6,4},{7,5},{8,10},{9,11},{10,... | collective-permute-start | bytes 798728 | tf_op jit(solution)/shard_map/ppermute | solution.py:37
  8.2 18.5 %collective-permute-start = (f32[8,8320]{1,0:T(8,128)S(1)}, f32[8,8320]{1,0:T(8,128)S(1)}, u32[]{:S(2)}, u32[]{:S(2)}) collective-permute-start(f32[8,8320]{1,0:T(8,128)S(1)} %get-tuple-element.20.refs_0_), channel_id=1, source_target_pairs={{0,1},{1,0},{2,3},{3,2},{4,5},{5,4},{6,7},{7,6},{8,9},{9,8},{10,11... | collective-permute-start | bytes 798728 | tf_op jit(solution)/shard_map/ppermute | solution.py:37
  8.7 3.9 %collective-permute-start.4 = (f32[8,2176]{1,0:T(8,128)S(1)}, f32[8,2176]{1,0:T(8,128)S(1)}, u32[]{:S(2)}, u32[]{:S(2)}) collective-permute-start(f32[8,2176]{1,0:T(8,128)S(1)} %get-tuple-element.25), channel_id=1, source_target_pairs={{0,4},{4,0},{8,12},{12,8},{16,20},{20,16},{24,28},{28,24},{1,5},{5... | collective-permute-start | bytes 208904 | tf_op jit(solution)/shard_map/ppermute | solution.py:37
  11.9 4.8 %collective-permute-start.5 = (f32[8,2176]{1,0:T(8,128)S(1)}, f32[8,2176]{1,0:T(8,128)S(1)}, u32[]{:S(2)}, u32[]{:S(2)}) collective-permute-start(f32[8,2176]{1,0:T(8,128)S(1)} %get-tuple-element.26), channel_id=1, source_target_pairs={{0,8},{4,12},{8,0},{12,4},{16,24},{20,28},{24,16},{28,20},{1,9},{5... | collective-permute-start | bytes 208904 | tf_op jit(solution)/shard_map/ppermute | solution.py:37
  12.6 4.5 %collective-permute-start.6 = (f32[8,2176]{1,0:T(8,128)S(1)}, f32[8,2176]{1,0:T(8,128)S(1)}, u32[]{:S(2)}, u32[]{:S(2)}) collective-permute-start(f32[8,2176]{1,0:T(8,128)S(1)} %get-tuple-element.27), channel_id=1, source_target_pairs={{0,12},{4,8},{8,4},{12,0},{16,28},{20,24},{24,20},{28,16},{1,13},{... | collective-permute-start | bytes 208904 | tf_op jit(solution)/shard_map/ppermute | solution.py:37
  16.7 1.7 %collective-permute-start.7 = (f32[8,2176]{1,0:T(8,128)S(1)}, f32[8,2176]{1,0:T(8,128)S(1)}, u32[]{:S(2)}, u32[]{:S(2)}) collective-permute-start(f32[8,2176]{1,0:T(8,128)S(1)} %get-tuple-element.28), channel_id=1, source_target_pairs={{0,4},{4,0},{8,12},{12,8},{16,20},{20,16},{24,28},{28,24},{1,5},{5... | collective-permute-start | bytes 208904 | tf_op jit(solution)/shard_map/ppermute | solution.py:37
  17.2 5.1 %collective-permute-start.8 = (f32[8,2176]{1,0:T(8,128)S(1)}, f32[8,2176]{1,0:T(8,128)S(1)}, u32[]{:S(2)}, u32[]{:S(2)}) collective-permute-start(f32[8,2176]{1,0:T(8,128)S(1)} %get-tuple-element.29), channel_id=1, source_target_pairs={{0,8},{4,12},{8,0},{12,4},{16,24},{20,28},{24,16},{28,20},{1,9},{5... | collective-permute-start | bytes 208904 | tf_op jit(solution)/shard_map/ppermute | solution.py:37
  18.4 4.6 %collective-permute-start.9 = (f32[8,2176]{1,0:T(8,128)S(1)}, f32[8,2176]{1,0:T(8,128)S(1)}, u32[]{:S(2)}, u32[]{:S(2)}) collective-permute-start(f32[8,2176]{1,0:T(8,128)S(1)} %get-tuple-element.30), channel_id=1, source_target_pairs={{0,12},{4,8},{8,4},{12,0},{16,28},{20,24},{24,20},{28,16},{1,13},{... | collective-permute-start | bytes 208904 | tf_op jit(solution)/shard_map/ppermute | solution.py:37
  23.1 7.3 %collective-permute-start.12 = (f32[8,4352]{1,0:T(8,128)S(1)}, f32[8,4352]{1,0:T(8,128)S(1)}, u32[]{:S(2)}, u32[]{:S(2)}) collective-permute-start(f32[8,4352]{1,0:T(8,128)S(1)} %pick.1.refs_0_), channel_id=1, source_target_pairs={{0,3},{1,2},{2,1},{3,0},{4,7},{5,6},{6,5},{7,4},{8,11},{9,10},{10,... | collective-permute-start | bytes 417800 | tf_op jit(solution)/shard_map/ppermute | solution.py:37
  25.7 7.1 %collective-permute-start.11 = (f32[8,4352]{1,0:T(8,128)S(1)}, f32[8,4352]{1,0:T(8,128)S(1)}, u32[]{:S(2)}, u32[]{:S(2)}) collective-permute-start(f32[8,4352]{1,0:T(8,128)S(1)} %pick.1.refs_0_), channel_id=1, source_target_pairs={{0,2},{1,3},{2,0},{3,1},{4,6},{5,7},{6,4},{7,5},{8,10},{9,11},{10,... | collective-permute-start | bytes 417800 | tf_op jit(solution)/shard_map/ppermute | solution.py:37
  26.2 6.7 %collective-permute-start.10 = (f32[8,4352]{1,0:T(8,128)S(1)}, f32[8,4352]{1,0:T(8,128)S(1)}, u32[]{:S(2)}, u32[]{:S(2)}) collective-permute-start(f32[8,4352]{1,0:T(8,128)S(1)} %pick.1.refs_0_), channel_id=1, source_target_pairs={{0,1},{1,0},{2,3},{3,2},{4,5},{5,4},{6,7},{7,6},{8,9},{9,8},{10,11... | collective-permute-start | bytes 417800 | tf_op jit(solution)/shard_map/ppermute | solution.py:37
